TPU v7x, 32 devices: a whole 2x2x4 slice. The times are simulated.
32 devices in a mesh: dp: 32 (over z, y, x, core).
Axes of the slice: x: 2, y: 2, z: 4, core: 2. Of those that a mesh axis runs over, the one named last changes fastest.
Arguments:
- tokens: bfloat16 [64, 1024, 768], P(None, 'dp'), may hold values from -6 to 6
- cotangent: bfloat16 [64, 1024, 768], P(None, 'dp'), may hold values from -6 to 6
- lengths: int32 [64], replicated, may hold values from 1 to 1024, 32768 in all
- order: int32 [64], replicated, may hold values from 0 to 63, each once
- query_weight: bfloat16 [768, 768], P('dp'), may hold values from -0.21875 to 0.21875
- query_bias: bfloat16 [768], P('dp'), may hold values from -3 to 3
- key_weight: bfloat16 [768, 768], P('dp'), may hold values from -0.21875 to 0.21875
- value_weight: bfloat16 [768, 768], P('dp'), may hold values from -0.21875 to 0.21875
- value_bias: bfloat16 [768], P('dp'), may hold values from -3 to 3
- output_weight: bfloat16 [768, 768], P('dp'), may hold values from -1.75 to 1.75
- output_bias: bfloat16 [768], P('dp'), may hold values from -3 to 3
- first_gain: bfloat16 [768], P('dp'), may hold values from 0.5 to 1.5
- first_shift: bfloat16 [768], P('dp'), may hold values from -3 to 3
- inner_weight: bfloat16 [768, 3072], P('dp'), may hold values from -0.21875 to 0.21875
- inner_bias: bfloat16 [3072], P('dp'), may hold values from -3 to 3
- outer_weight: bfloat16 [3072, 768], P('dp'), may hold values from -0.109375 to 0.109375
- outer_bias: bfloat16 [768], P('dp'), may hold values from -3 to 3
- second_gain: bfloat16 [768], P('dp'), may hold values from 0.5 to 1.5
- second_shift: bfloat16 [768], P('dp'), may hold values from -3 to 3
Outputs:
- output: bfloat16 [64, 1024, 768], P(None, 'dp')
- input_gradient: bfloat16 [64, 1024, 768], P(None, 'dp')
- query_weight_gradient: float32 [768, 768], P('dp')
- query_bias_gradient: float32 [768], P('dp')
- key_weight_gradient: float32 [768, 768], P('dp')
- value_weight_gradient: float32 [768, 768], P('dp')
- value_bias_gradient: float32 [768], P('dp')
- output_weight_gradient: float32 [768, 768], P('dp')
- output_bias_gradient: float32 [768], P('dp')
- first_gain_gradient: float32 [768], P('dp')
- first_shift_gradient: float32 [768], P('dp')
- inner_weight_gradient: float32 [768, 3072], P('dp')
- inner_bias_gradient: float32 [3072], P('dp')
- outer_weight_gradient: float32 [3072, 768], P('dp')
- outer_bias_gradient: float32 [768], P('dp')
- second_gain_gradient: float32 [768], P('dp')
- second_shift_gradient: float32 [768], P('dp')
Inputs may be any that keep to these rules, and one draw needn't show every extreme that they name: The lengths add up to 32768, and some sequence has exactly 1024 tokens. `order`: every sequence number appears once; slots k * 2 to (k + 1) * 2 - 1 belong to device k.
All inputs are finite; a program needn't handle non-finite values.
Results may differ from a plain program's by a relative error of at most 0.015.
Values may be sent and summed in bfloat16 or wider, within the bound.
A program may use at most 448 MiB of HBM per device.

v0:
```python
import jax
import jax.numpy as jnp
from jax import lax
from jax.sharding import PartitionSpec as P

HEADS = 12
MB = 2


epsilon = 1e-05


def matmul(left, right):
    return jnp.dot(left, right, preferred_element_type=jnp.float32)


def matmul_tn(left, right):
    return lax.dot_general(
        left, right, (((0,), (0,)), ((), ())), preferred_element_type=jnp.float32
    )


def matmul_nt(left, right):
    return lax.dot_general(
        left, right, (((1,), (1,)), ((), ())), preferred_element_type=jnp.float32
    )


def normalize(hidden):
    center = hidden - jnp.mean(hidden, axis=-1, keepdims=True)
    scale = lax.rsqrt(jnp.mean(center * center, axis=-1, keepdims=True) + epsilon)
    return (center * scale, scale)


def norm_back(grad_norm, normed, scale):
    first = jnp.mean(grad_norm, axis=-1, keepdims=True)
    second = jnp.mean(grad_norm * normed, axis=-1, keepdims=True)
    return scale * (grad_norm - first - normed * second)


def gelu_exact(inner):
    return jax.nn.gelu(inner, approximate=False)


def attend(queries, keys, values, length):
    span = keys.shape[0]
    width = queries.shape[1] // HEADS
    factor = width ** (-0.5)
    block = min(512, span)
    key_heads = keys.reshape(span, HEADS, width)
    value_heads = values.reshape(span, HEADS, width)
    valid = lax.broadcasted_iota(jnp.int32, (1, 1, span), 2) < length
    contexts = []
    totals = []
    for start in range(0, span, block):
        query_block = queries[start : start + block].reshape(block, HEADS, width)
        scores = (
            jnp.einsum("qhd,khd->hqk", query_block, key_heads, preferred_element_type=jnp.float32)
            * factor
        )
        scores = jnp.where(valid, scores, -1e30)
        top = jnp.max(scores, axis=-1, keepdims=True)
        expanded = jnp.exp(scores - top)
        summed = jnp.sum(expanded, axis=-1, keepdims=True)
        probs = (expanded / summed).astype(jnp.bfloat16)
        context = jnp.einsum("hqk,khd->qhd", probs, value_heads, preferred_element_type=jnp.float32)
        contexts.append(context.reshape(block, HEADS * width).astype(jnp.bfloat16))
        totals.append(top + jnp.log(summed))
    return (jnp.concatenate(contexts, axis=0), jnp.concatenate(totals, axis=1))


def attend_back(queries, keys, values, length, totals, grad_context):
    span = keys.shape[0]
    width = queries.shape[1] // HEADS
    factor = width ** (-0.5)
    block = min(512, span)
    key_heads = keys.reshape(span, HEADS, width)
    value_heads = values.reshape(span, HEADS, width)
    valid = lax.broadcasted_iota(jnp.int32, (1, 1, span), 2) < length
    key_grad = jnp.zeros((span, HEADS, width), jnp.float32)
    value_grad = jnp.zeros((span, HEADS, width), jnp.float32)
    query_grads = []
    for start in range(0, span, block):
        query_block = queries[start : start + block].reshape(block, HEADS, width)
        grad_block = grad_context[start : start + block].reshape(block, HEADS, width)
        scores = (
            jnp.einsum("qhd,khd->hqk", query_block, key_heads, preferred_element_type=jnp.float32)
            * factor
        )
        scores = jnp.where(valid, scores, -1e30)
        probs = jnp.exp(scores - totals[:, start : start + block])
        low_probs = probs.astype(jnp.bfloat16)
        value_grad = value_grad + jnp.einsum(
            "hqk,qhd->khd", low_probs, grad_block, preferred_element_type=jnp.float32
        )
        grad_probs = jnp.einsum(
            "qhd,khd->hqk", grad_block, value_heads, preferred_element_type=jnp.float32
        )
        inner_sum = jnp.sum(probs * grad_probs, axis=-1, keepdims=True)
        grad_scores = (probs * (grad_probs - inner_sum)).astype(jnp.bfloat16)
        query_grad = (
            jnp.einsum("hqk,khd->qhd", grad_scores, key_heads, preferred_element_type=jnp.float32)
            * factor
        )
        query_grads.append(query_grad.reshape(block, HEADS * width).astype(jnp.bfloat16))
        key_grad = (
            key_grad
            + jnp.einsum(
                "hqk,qhd->khd", grad_scores, query_block, preferred_element_type=jnp.float32
            )
            * factor
        )
    return (
        jnp.concatenate(query_grads, axis=0),
        key_grad.reshape(span, HEADS * width).astype(jnp.bfloat16),
        value_grad.reshape(span, HEADS * width).astype(jnp.bfloat16),
    )


def forward(rows, batch_lengths, full):
    (
        query_weight,
        query_bias,
        key_weight,
        value_weight,
        value_bias,
        output_weight,
        output_bias,
        first_gain,
        first_shift,
        inner_weight,
        inner_bias,
        outer_weight,
        outer_bias,
        second_gain,
        second_shift,
    ) = full
    count, span, width = rows.shape
    flat = rows.reshape(count * span, width)
    queries = (matmul(flat, query_weight) + query_bias.astype(jnp.float32)).astype(jnp.bfloat16)
    keys = matmul(flat, key_weight).astype(jnp.bfloat16)
    values = (matmul(flat, value_weight) + value_bias.astype(jnp.float32)).astype(jnp.bfloat16)
    context, total = attend(queries, keys, values, batch_lengths[0])
    contexts = context
    totals = [total]
    context = contexts
    attended = matmul(context, output_weight) + output_bias.astype(jnp.float32)
    first_normed, first_scale = normalize(flat.astype(jnp.float32) + attended)
    mixed = first_normed * first_gain.astype(jnp.float32) + first_shift.astype(jnp.float32)
    low_mixed = mixed.astype(jnp.bfloat16)
    inner = matmul(low_mixed, inner_weight) + inner_bias.astype(jnp.float32)
    activated = gelu_exact(inner).astype(jnp.bfloat16)
    branch = matmul(activated, outer_weight) + outer_bias.astype(jnp.float32)
    second_normed, second_scale = normalize(mixed + branch)
    positions = lax.broadcasted_iota(jnp.int32, (count, span), 1)
    live = (positions < batch_lengths[:, None]).reshape(count * span, 1).astype(jnp.float32)
    result = (
        second_normed * second_gain.astype(jnp.float32) + second_shift.astype(jnp.float32)
    ) * live
    saved = (
        flat,
        queries,
        keys,
        values,
        totals,
        context,
        first_normed,
        first_scale,
        low_mixed,
        inner,
        activated,
        second_normed,
        second_scale,
        live,
    )
    return (result.astype(jnp.bfloat16).reshape(count, span, width), saved)


def backward(grad_rows, batch_lengths, full, saved):
    (
        query_weight,
        query_bias,
        key_weight,
        value_weight,
        value_bias,
        output_weight,
        output_bias,
        first_gain,
        first_shift,
        inner_weight,
        inner_bias,
        outer_weight,
        outer_bias,
        second_gain,
        second_shift,
    ) = full
    (
        flat,
        queries,
        keys,
        values,
        totals,
        context,
        first_normed,
        first_scale,
        low_mixed,
        inner,
        activated,
        second_normed,
        second_scale,
        live,
    ) = saved
    count, span, width = grad_rows.shape
    grad_out = grad_rows.reshape(count * span, width).astype(jnp.float32) * live
    second_gain_grad = jnp.sum(grad_out * second_normed, axis=0)
    second_shift_grad = jnp.sum(grad_out, axis=0)
    grad_second = norm_back(grad_out * second_gain.astype(jnp.float32), second_normed, second_scale)
    grad_branch = grad_second.astype(jnp.bfloat16)
    outer_bias_grad = jnp.sum(grad_branch.astype(jnp.float32), axis=0)
    outer_weight_grad = matmul_tn(activated, grad_branch)
    _, gelu_pull = jax.vjp(gelu_exact, inner)
    (grad_inner,) = gelu_pull(matmul_nt(grad_branch, outer_weight))
    grad_inner = grad_inner.astype(jnp.bfloat16)
    inner_bias_grad = jnp.sum(grad_inner.astype(jnp.float32), axis=0)
    inner_weight_grad = matmul_tn(low_mixed, grad_inner)
    grad_mixed = grad_second + matmul_nt(grad_inner, inner_weight)
    first_gain_grad = jnp.sum(grad_mixed * first_normed, axis=0)
    first_shift_grad = jnp.sum(grad_mixed, axis=0)
    grad_first = norm_back(grad_mixed * first_gain.astype(jnp.float32), first_normed, first_scale)
    grad_attended = grad_first.astype(jnp.bfloat16)
    output_bias_grad = jnp.sum(grad_attended.astype(jnp.float32), axis=0)
    output_weight_grad = matmul_tn(context, grad_attended)
    grad_context = matmul_nt(grad_attended, output_weight).astype(jnp.bfloat16)
    query_grad, key_grad, value_grad = attend_back(
        queries, keys, values, batch_lengths[0], totals[0], grad_context
    )
    query_weight_grad = matmul_tn(flat, query_grad)
    query_bias_grad = jnp.sum(query_grad.astype(jnp.float32), axis=0)
    key_weight_grad = matmul_tn(flat, key_grad)
    value_weight_grad = matmul_tn(flat, value_grad)
    value_bias_grad = jnp.sum(value_grad.astype(jnp.float32), axis=0)
    grad_input = (
        grad_first
        + matmul_nt(query_grad, query_weight)
        + matmul_nt(key_grad, key_weight)
        + matmul_nt(value_grad, value_weight)
    )
    grads = (
        query_weight_grad,
        query_bias_grad,
        key_weight_grad,
        value_weight_grad,
        value_bias_grad,
        output_weight_grad,
        output_bias_grad,
        first_gain_grad,
        first_shift_grad,
        inner_weight_grad,
        inner_bias_grad,
        outer_weight_grad,
        outer_bias_grad,
        second_gain_grad,
        second_shift_grad,
    )
    return (grads, grad_input.astype(jnp.bfloat16).reshape(count, span, width))


def fetch(shards):
    return (
        lax.all_gather(shards[0], "dp", axis=0, tiled=True),
        lax.all_gather(shards[1], "dp", axis=0, tiled=True),
        lax.all_gather(shards[2], "dp", axis=0, tiled=True),
        lax.all_gather(shards[3], "dp", axis=0, tiled=True),
        lax.all_gather(shards[4], "dp", axis=0, tiled=True),
        lax.all_gather(shards[5], "dp", axis=0, tiled=True),
        lax.all_gather(shards[6], "dp", axis=0, tiled=True),
        lax.all_gather(shards[7], "dp", axis=0, tiled=True),
        lax.all_gather(shards[8], "dp", axis=0, tiled=True),
        lax.all_gather(shards[9], "dp", axis=0, tiled=True),
        lax.all_gather(shards[10], "dp", axis=0, tiled=True),
        lax.all_gather(shards[11], "dp", axis=0, tiled=True),
        lax.all_gather(shards[12], "dp", axis=0, tiled=True),
        lax.all_gather(shards[13], "dp", axis=0, tiled=True),
        lax.all_gather(shards[14], "dp", axis=0, tiled=True),
    )


def body(
    tokens,
    cotangent,
    lengths,
    order,
    query_weight,
    query_bias,
    key_weight,
    value_weight,
    value_bias,
    output_weight,
    output_bias,
    first_gain,
    first_shift,
    inner_weight,
    inner_bias,
    outer_weight,
    outer_bias,
    second_gain,
    second_shift,
):
    shards = (
        query_weight,
        query_bias,
        key_weight,
        value_weight,
        value_bias,
        output_weight,
        output_bias,
        first_gain,
        first_shift,
        inner_weight,
        inner_bias,
        outer_weight,
        outer_bias,
        second_gain,
        second_shift,
    )
    devices = lax.axis_size("dp")
    device = lax.axis_index("dp")
    per_device = tokens.shape[0] // devices
    per_batch = per_device // MB
    dealt = jnp.take(tokens, order, axis=0)
    rows_in, grads_in = (
        lax.all_to_all(dealt, "dp", split_axis=0, concat_axis=1, tiled=True),
        lax.all_to_all(cotangent, "dp", split_axis=0, concat_axis=1, tiled=True),
    )
    dealt_lengths = jnp.take(lengths, order)
    my_lengths = lax.dynamic_slice_in_dim(dealt_lengths, device * per_device, per_device)
    results = []
    input_grads = []
    summed = None
    for batch in range(MB):
        part = slice(batch * per_batch, (batch + 1) * per_batch)
        batch_lengths = my_lengths[part]
        full = fetch(shards)
        result, saved = forward(rows_in[part], batch_lengths, full)
        results.append(result)
        full = fetch(shards)
        grads, grad_input = backward(grads_in[part], batch_lengths, full, saved)
        input_grads.append(grad_input)
        pieces = (
            lax.psum_scatter(grads[0], "dp", scatter_dimension=0, tiled=True),
            lax.psum_scatter(grads[1], "dp", scatter_dimension=0, tiled=True),
            lax.psum_scatter(grads[2], "dp", scatter_dimension=0, tiled=True),
            lax.psum_scatter(grads[3], "dp", scatter_dimension=0, tiled=True),
            lax.psum_scatter(grads[4], "dp", scatter_dimension=0, tiled=True),
            lax.psum_scatter(grads[5], "dp", scatter_dimension=0, tiled=True),
            lax.psum_scatter(grads[6], "dp", scatter_dimension=0, tiled=True),
            lax.psum_scatter(grads[7], "dp", scatter_dimension=0, tiled=True),
            lax.psum_scatter(grads[8], "dp", scatter_dimension=0, tiled=True),
            lax.psum_scatter(grads[9], "dp", scatter_dimension=0, tiled=True),
            lax.psum_scatter(grads[10], "dp", scatter_dimension=0, tiled=True),
            lax.psum_scatter(grads[11], "dp", scatter_dimension=0, tiled=True),
            lax.psum_scatter(grads[12], "dp", scatter_dimension=0, tiled=True),
            lax.psum_scatter(grads[13], "dp", scatter_dimension=0, tiled=True),
            lax.psum_scatter(grads[14], "dp", scatter_dimension=0, tiled=True),
        )
        if summed is None:
            summed = pieces
        else:
            summed = tuple((left + right for left, right in zip(summed, pieces)))
    output, input_gradient = (
        lax.all_to_all(
            jnp.concatenate(results, axis=0), "dp", split_axis=1, concat_axis=0, tiled=True
        ),
        lax.all_to_all(
            jnp.concatenate(input_grads, axis=0), "dp", split_axis=1, concat_axis=0, tiled=True
        ),
    )
    return (
        output,
        input_gradient,
        summed[0],
        summed[1],
        summed[2],
        summed[3],
        summed[4],
        summed[5],
        summed[6],
        summed[7],
        summed[8],
        summed[9],
        summed[10],
        summed[11],
        summed[12],
        summed[13],
        summed[14],
    )


def solution(mesh):
    in_specs = (
        P(None, "dp", None),
        P(None, "dp", None),
        P(),
        P(),
        P("dp", None),
        P("dp"),
        P("dp", None),
        P("dp", None),
        P("dp"),
        P("dp", None),
        P("dp"),
        P("dp"),
        P("dp"),
        P("dp", None),
        P("dp"),
        P("dp", None),
        P("dp"),
        P("dp"),
        P("dp"),
    )
    out_specs = (
        P(None, "dp", None),
        P(None, "dp", None),
        P("dp", None),
        P("dp"),
        P("dp", None),
        P("dp", None),
        P("dp"),
        P("dp", None),
        P("dp"),
        P("dp"),
        P("dp"),
        P("dp", None),
        P("dp"),
        P("dp", None),
        P("dp"),
        P("dp"),
        P("dp"),
    )
    return jax.shard_map(body, mesh=mesh, in_specs=in_specs, out_specs=out_specs, check_vma=False)
```

profile of v0, /device:TPU:0, one launch (start us, length us, event | category | flops | bytes accessed | tf_op | source)
XLA Modules:
  0.0 1352.4 jit_solution(94236992821572649)
XLA Ops:
  15.1 3.9 broadcast_select_fusion
  19.1 7.3 all-to-all-start
  29.2 94.9 %all-reduce.19 = (bf16[768]{0:T(1024)(128)(2,1)S(1)}, bf16[768]{0:T(1024)(128)(2,1)S(1)}, bf16[768]{0:T(1024)(128)(2,1)S(1)}, bf16[768]{0:T(1024)(128)(2,1)S(1)}...) all-reduce(bf16[768]{0:T(1024)(128)(2,1)S(1)} %dynamic-update-slice, ...), channel_id=1, replica_groups=mesh['dp'=32] {'dp'}, use_global_device_ids=true, to_apply=%add.2 | all-reduce | flops 9216 | bytes 36864
  135.2 4.0 all-to-all-start.2
  147.0 3.7 convolution_convert_fusion.2
  150.7 10.2 fusion.38
  160.9 22.1 %fusion.2 = (f32[12,512]{1,0:T(8,128)S(1)}, f32[12,512]{1,0:T(8,128)S(1)}, f32[12,512,1024]{2,1,0:T(8,128)}) fusion(f32[12,512]{1,0:T(8,128)S(1)} %get-tuple-element.111, f32[12,512,1024]{2,1,0:T(8,128)} %get-tuple-element.112, pred[1024]{0:T(1024)(128)(4,1)S(1)} %iota_compare_fusion, bf16[512,12,64]{0,2,1:T(8,128)(2,1)S(1)} %bitcast.217, ...), kind=kOutput, calls=%fused_computation.28 | convolution fusion | flops 849334272 | bytes 52765696 | tf_op jit(solution)/shard_map/qhd,khd->hqk/dot_general | solution.py:58
  183.0 11.3 fusion.3
  195.0 12.5 all-gather.7.cloned.1.call-done
  210.2 12.6 fusion.51
  222.8 12.1 fusion.50
  242.5 10.4 fusion.36
  252.9 22.3 %fusion = (f32[12,512]{1,0:T(8,128)S(1)}, f32[12,512]{1,0:T(8,128)S(1)}, f32[12,512,1024]{2,1,0:T(8,128)}) fusion(f32[12,512]{1,0:T(8,128)S(1)} %get-tuple-element.106, f32[12,512,1024]{2,1,0:T(8,128)} %get-tuple-element.107, pred[1024]{0:T(1024)(128)(4,1)S(1)} %iota_compare_fusion.1, bf16[512,12,64]{0,2,1:T(8,128)(2,1)S(1)} %bitcast.219, ...), kind=kOutput, calls=%fused_computation.26 | convolution fusion | flops 849334272 | bytes 52765696 | tf_op jit(solution)/shard_map/qhd,khd->hqk/dot_general | solution.py:58
  275.2 11.4 fusion.1
  288.8 12.7 fusion.53
  301.5 12.1 fusion.52
  313.6 4.4 slice_convert_fusion.1
  318.0 3.5 multiply_reduce_fusion.19
  322.8 3.5 copy.91
  329.0 3.9 fusion.113
  341.5 7.7 fusion.98
  349.2 4.5 copy-done.17
  353.8 68.3 %multiply_convert_fusion.5 = (bf16[1024,3072]{1,0:T(8,128)(2,1)}, f32[1024,3072]{1,0:T(8,128)}, bf16[1024,3072]{1,0:T(8,128)(2,1)}, f32[1024,3072]{1,0:T(8,128)}, f32[1024,3072]{1,0:T(8,128)}) fusion(f32[3072]{0:T(1024)S(1)} %copy-done.111, f32[1024,3072]{1,0:T(8,128)S(1)} %fusion.98, bf16[768,3072]{1,0:T(8,128)(2,1)S(1)} %copy-done.40, ...), kind=kOutput, calls=%fused_computation.63 | convolution fusion | flops 5247074304 | bytes 69218304 | tf_op jit(solution)/shard_map/dot_general | solution.py:14
  422.2 10.0 fusion.114
  434.1 7.8 fusion.115
  443.8 3.1 multiply_reduce_fusion.5
  446.9 5.9 convert_reduce_fusion.2
  452.9 19.6 %convert_reduce_fusion.1 = (f32[3072]{0:T(1024)}, bf16[1024,3072]{1,0:T(8,128)(2,1)}) fusion(f32[1024,3072]{1,0:T(8,128)} %get-tuple-element.70, bf16[3072,768]{1,0:T(8,128)(2,1)} %all-gather.17.cloned.1.call-done, f32[1024,768]{0,1:T(8,128)} %get-tuple-element.93, f32[1024,3072]{1,0:T(8,128)} %get-tuple-element.116, f32[3072]{0:T(1024)S(1)} %copy-done.111), kind=kOutput, calls=%fused_computation.43 | convolution fusion | flops 4886098944 | bytes 39346176 | tf_op jit(solution)/shard_map/dot_general | solution.py:24
  472.5 12.6 multiply_reduce_fusion.7
  485.0 19.8 %convert_reduce_fusion = (f32[3072]{0:T(1024)}, bf16[1024,3072]{1,0:T(8,128)(2,1)}) fusion(f32[1024,3072]{1,0:T(8,128)} %get-tuple-element.90, bf16[3072,768]{1,0:T(8,128)(2,1)} %all-gather.17.cloned.1.call-done, f32[1024,768]{0,1:T(8,128)} %get-tuple-element.62, f32[1024,3072]{1,0:T(8,128)} %copy-done.17, f32[3072]{0:T(1024)S(1)} %copy-done.111), kind=kOutput, calls=%fused_computation.42 | convolution fusion | flops 4886098944 | bytes 39346176 | tf_op jit(solution)/shard_map/dot_general | solution.py:24
  504.8 12.7 convert_reduce_fusion.5
  522.5 2.8 convolution_add_fusion.4
  525.8 3.4 convolution_convert_fusion
  534.6 10.4 fusion.116
  545.0 10.9 fusion.14
  555.9 12.4 convert_reduce_fusion.7
  568.2 2.8 fusion.121
  571.1 10.2 fusion.118
  581.3 36.3 %multiply_reduce_fusion.2 = (f32[12,512]{1,0:T(8,128)S(1)}, f32[12,512]{1,0:T(8,128)S(1)}, f32[12,512,1024]{2,1,0:T(8,128)}) fusion(f32[12,512]{1,0:T(8,128)S(1)} %copy-done.83, f32[12,512,1024]{2,1,0:T(8,128)} %get-tuple-element.108, pred[1024]{0:T(1024)(128)(4,1)S(1)} %copy-done.110, f32[12,512,1024]{2,1,0:T(8,128)} %fusion.116, ...), kind=kOutput, calls=%fused_computation.9 | convolution fusion | flops 868208640 | bytes 103121920 | tf_op jit(solution)/shard_map/qhd,khd->hqk/dot_general | solution.py:96
  617.6 41.7 %multiply_convert_fusion.2 = (bf16[12,512,1024]{2,1,0:T(8,128)(2,1)}, bf16[12,512,1024]{2,1,0:T(8,128)(2,1)}) fusion(f32[12,512,1024]{2,1,0:T(8,128)} %get-tuple-element.124, f32[12,512]{1,0:T(8,128)S(1)} %get-tuple-element.35, f32[12,512]{1,0:T(8,128)S(1)} %copy-done.83, f32[12,512,1024]{2,1,0:T(8,128)} %get-tuple-element.108, ...), kind=kLoop, calls=%fused_computation.8 | loop fusion | flops 75497472 | bytes 125928448 | tf_op jit(solution)/shard_map/convert_element_type | solution.py:100
  659.3 6.9 fusion.117
  666.3 10.7 fusion.10
  677.0 12.3 convert_reduce_fusion.6
  690.5 2.8 convolution_add_fusion.5
  693.3 36.1 %multiply_reduce_fusion = (f32[12,512]{1,0:T(8,128)S(1)}, f32[12,512]{1,0:T(8,128)S(1)}, f32[12,512,1024]{2,1,0:T(8,128)}) fusion(f32[12,512]{1,0:T(8,128)S(1)} %copy-done.81, f32[12,512,1024]{2,1,0:T(8,128)} %get-tuple-element.113, pred[1024]{0:T(1024)(128)(4,1)S(1)} %copy-done.108, f32[12,512,1024]{2,1,0:T(8,128)} %fusion.118, ...), kind=kOutput, calls=%fused_computation.3 | convolution fusion | flops 868208640 | bytes 103121920 | tf_op jit(solution)/shard_map/qhd,khd->hqk/dot_general | solution.py:96
  729.5 7.1 multiply_convert_fusion.7
  736.7 43.5 %multiply_convert_fusion = (bf16[12,512,1024]{2,1,0:T(8,128)(2,1)}, bf16[12,512,1024]{2,1,0:T(8,128)(2,1)}) fusion(f32[12,512,1024]{2,1,0:T(8,128)} %get-tuple-element.123, f32[12,512]{1,0:T(8,128)S(1)} %get-tuple-element.37, f32[12,512]{1,0:T(8,128)S(1)} %copy-done.81, f32[12,512,1024]{2,1,0:T(8,128)} %get-tuple-element.113, ...), kind=kLoop, calls=%fused_computation.2 | loop fusion | flops 75497472 | bytes 125928448 | tf_op jit(solution)/shard_map/convert_element_type | solution.py:100
  781.7 7.2 fusion.119
  795.5 9.6 multiply_convert_fusion.12
  805.3 8.7 multiply_convert_fusion.13
  815.8 8.5 multiply_convert_fusion.10
  824.3 8.9 multiply_convert_fusion.11
  837.2 8.5 fusion.78
  845.7 11.0 convolution_add_fusion
  857.4 8.8 fusion.100
  866.2 10.6 convolution_add_fusion.1
  879.0 5.6 copy.88
  884.6 5.2 all-to-all-start.1
  902.7 5.9 copy.101
  908.7 58.7 %all-to-all-done.1 = bf16[2,1024,768]{2,0,1:T(2,128)(2,1)} async-done(((bf16[2,1024,768]{2,0,1:T(2,128)(2,1)}), bf16[2,1024,768]{2,0,1:T(2,128)(2,1)}, u32[]{:S(2)}, u32[]{:S(2)}) %all-to-all-start.1) | async-done | bytes 3145760 | tf_op jit(solution)/shard_map/all_to_all | solution.py:371
  967.4 3.4 all-to-all-start.3
  974.5 98.4 %all-reduce.18 = (f32[768]{0:T(1024)S(1)}, f32[768]{0:T(1024)S(1)}, f32[768]{0:T(1024)S(1)}, f32[768]{0:T(1024)S(1)}, f32[768]{0:T(1024)S(1)}, /*index=5*/f32[30...) all-reduce(f32[768]{0:T(1024)S(1)} %add.402, ...), channel_id=18, replica_groups=mesh['dp'=32] {'dp'}, use_global_device_ids=true, to_apply=%region_31.32.clone | all-reduce | flops 9216 | bytes 73728
  1084.9 118.3 %reduce-scatter.17.cloned.1.call-done = f32[96,768]{1,0:T(8,128)} async-done(((f32[3072,768]{1,0:T(8,128)}), f32[96,768]{1,0:T(8,128)}) %reduce-scatter.17.cloned.1.call-update) | async-done | bytes 294928 | tf_op jit(solution)/shard_map/reduce_scatter | solution.py:361
  1203.3 141.8 %reduce-scatter.15.cloned.1.call-done = f32[24,3072]{1,0:T(8,128)} async-done(((f32[768,3072]{1,0:T(8,128)}), f32[24,3072]{1,0:T(8,128)}) %reduce-scatter.15.cloned.1.call-update) | async-done | bytes 294928 | tf_op jit(solution)/shard_map/reduce_scatter | solution.py:359
  (453 shorter events, 115.8 us)
Async XLA Ops:
  7.2 136.9 %all-gather.9.cloned.1.call-start = ((), (), s32[]{:S(2)}) async-start(), calls=%async_computation.11 | async-start | bytes 1216512 | tf_op jit(solution)/shard_map/all_gather | solution.py:270
  7.9 139.0 %all-gather.11.cloned.1.call-start = ((), (), s32[]{:S(2)}) async-start(), calls=%async_computation.12 | async-start | bytes 1216512 | tf_op jit(solution)/shard_map/all_gather | solution.py:272
  8.7 198.8 %all-gather.7.cloned.1.call-start = ((), (), s32[]{:S(2)}) async-start(), calls=%async_computation.10 | async-start | bytes 1216512 | tf_op jit(solution)/shard_map/all_gather | solution.py:273
  9.4 319.5 %all-gather.13.cloned.1.call-start = ((), (), s32[]{:S(2)}) async-start(), calls=%async_computation.13 | async-start | bytes 1216512 | tf_op jit(solution)/shard_map/all_gather | solution.py:275
  10.0 331.5 %all-gather.15.cloned.1.call-start = ((), (), s32[]{:S(2)}) async-start(), calls=%async_computation.14 | async-start | bytes 4866048 | tf_op jit(solution)/shard_map/all_gather | solution.py:279
  19.1 116.1 %all-to-all-start = ((bf16[64,32,768]{2,1,0:T(8,128)(2,1)}), bf16[64,32,768]{2,1,0:T(8,128)(2,1)S(1)}, u32[]{:S(2)}, u32[]{:S(2)}) async-start(bf16[64,32,768]{2,1,0:T(8,128)(2,1)} %broadcast_select_fusion), calls=%async_computation | async-start | bytes 6291456 | tf_op jit(solution)/shard_map/all_to_all | solution.py:332
  26.4 395.7 %all-gather.17.cloned.1.call-start = ((), (), s32[]{:S(2)}) async-start(), calls=%async_computation.15 | async-start | bytes 4866048 | tf_op jit(solution)/shard_map/all_gather | solution.py:281
  129.5 172.0 %copy-start.109 = (pred[1024]{0:T(1024)(128)(4,1)}, pred[1024]{0:T(1024)(128)(4,1)S(1)}, u32[]{:S(2)}) copy-start(pred[1024]{0:T(1024)(128)(4,1)S(1)} %iota_compare_fusion.1) | copy-start | bytes 3076
  130.2 92.6 %copy-start.107 = (pred[1024]{0:T(1024)(128)(4,1)}, pred[1024]{0:T(1024)(128)(4,1)S(1)}, u32[]{:S(2)}) copy-start(pred[1024]{0:T(1024)(128)(4,1)S(1)} %iota_compare_fusion) | copy-start | bytes 3076
  135.2 178.4 %all-to-all-start.2 = ((bf16[64,32,768]{2,1,0:T(8,128)(2,1)}), bf16[64,32,768]{2,1,0:T(8,128)(2,1)}, u32[]{:S(2)}, u32[]{:S(2)}) async-start(bf16[64,32,768]{2,1,0:T(8,128)(2,1)} %param.20), calls=%async_computation.2 | async-start | bytes 6291456 | tf_op jit(solution)/shard_map/all_to_all | solution.py:333
  139.2 945.7 %reduce-scatter.13.cloned.1.call-start = ((), (), s32[]{:S(2)}) async-start(), calls=%async_computation.19 | async-start | bytes 2433024 | tf_op jit(solution)/shard_map/reduce_scatter | solution.py:355
  146.9 14.0 %copy-start.37 = (bf16[512,768]{0,1:T(8,128)(2,1)}, bf16[512,768]{0,1:T(8,128)(2,1)S(1)}, u32[]{:S(2)}) copy-start(bf16[512,768]{0,1:T(8,128)(2,1)S(1)} %get-tuple-element.87) | copy-start | bytes 2359300
  183.0 24.5 %copy-start.27 = (bf16[1,32,32,768]{3,2,0,1:T(8,128)(2,1)S(1)}, bf16[1,32,32,768]{3,2,0,1:T(8,128)(2,1)}, u32[]{:S(2)}) copy-start(bf16[1,32,32,768]{3,2,0,1:T(8,128)(2,1)} %get-tuple-element.80) | copy-start | bytes 4718596
  210.2 12.6 copy-start.13
  222.8 12.1 copy-start.31
  241.0 11.9 copy-start.39
  275.2 12.0 copy-start.33
  275.2 12.0 copy-start.41
  288.7 12.8 copy-start.15
  341.5 12.3 copy-start.111
  341.5 12.3 copy-start.40
  341.5 12.3 copy-start.62
  353.8 68.4 %copy-start.19 = (f32[1024,768]{0,1:T(8,128)S(1)}, f32[1024,768]{0,1:T(8,128)}, u32[]{:S(2)}) copy-start(f32[1024,768]{0,1:T(8,128)} %copy-done.18) | copy-start | bytes 9437188
  353.8 68.4 %copy-start.70 = (f32[768]{0:T(1024)S(1)}, f32[768]{0:T(1024)}, u32[]{:S(2)}) copy-start(f32[768]{0:T(1024)} %convert_element_type.355) | copy-start | bytes 9220
  353.8 68.4 %copy-start.76 = (f32[768]{0:T(1024)S(1)}, f32[768]{0:T(1024)}, u32[]{:S(2)}) copy-start(f32[768]{0:T(1024)} %convert_element_type.356) | copy-start | bytes 9220
  353.8 68.4 %copy-start.92 = (f32[1024]{0:T(1024)S(1)}, f32[1024]{0:T(1024)}, u32[]{:S(2)}) copy-start(f32[1024]{0:T(1024)} %copy-done.91) | copy-start | bytes 12292
  353.8 68.4 %copy-start.104 = (f32[1024]{0:T(1024)S(1)}, f32[1024]{0:T(1024)}, u32[]{:S(2)}) copy-start(f32[1024]{0:T(1024)} %copy-done.103) | copy-start | bytes 12292
  353.8 68.4 %copy-start.121 = (f32[768]{0:T(1024)S(1)}, f32[768]{0:T(1024)}, u32[]{:S(2)}) copy-start(f32[768]{0:T(1024)} %convert_element_type.360) | copy-start | bytes 9220
  504.8 12.7 copy-start.140
  504.8 12.7 copy-start.142
  525.4 559.6 %reduce-scatter.11.cloned.1.call-start = ((), (), s32[]{:S(2)}) async-start(), calls=%async_computation.18 | async-start | bytes 2433024 | tf_op jit(solution)/shard_map/reduce_scatter | solution.py:353
  531.4 39.6 %copy-start.24 = (bf16[512,768]{0,1:T(8,128)(2,1)}, bf16[512,768]{0,1:T(8,128)(2,1)S(1)}, u32[]{:S(2)}) copy-start(bf16[512,768]{0,1:T(8,128)(2,1)S(1)} %get-tuple-element.83) | copy-start | bytes 2359300
  533.0 12.0 copy-start.48
  545.0 10.9 copy-start.84
  555.9 12.4 copy-start.34
  617.6 41.7 %copy-start.23 = (bf16[512,768]{0,1:T(8,128)(2,1)S(1)}, bf16[512,768]{0,1:T(8,128)(2,1)}, u32[]{:S(2)}) copy-start(bf16[512,768]{0,1:T(8,128)(2,1)} %copy-done.22) | copy-start | bytes 2359300
  666.3 10.7 copy-start.25
  677.0 13.5 copy-start.28
  677.0 13.5 copy-start.143
  729.4 355.5 %reduce-scatter.9.cloned.1.call-start = ((), (), s32[]{:S(2)}) async-start(), calls=%async_computation.17 | async-start | bytes 2433024 | tf_op jit(solution)/shard_map/reduce_scatter | solution.py:352
  736.6 43.5 %copy-start.43 = (bf16[12,64,1024]{2,1,0:T(8,128)(2,1)}, bf16[12,64,1024]{2,1,0:T(8,128)(2,1)S(1)}, u32[]{:S(2)}) copy-start(bf16[12,64,1024]{2,1,0:T(8,128)(2,1)S(1)} %multiply_convert_fusion.7) | copy-start | bytes 4718596
  736.6 43.5 %copy-start.35 = (bf16[1,32,32,768]{3,2,0,1:T(8,128)(2,1)S(1)}, bf16[1,32,32,768]{3,2,0,1:T(8,128)(2,1)}, u32[]{:S(2)}) copy-start(bf16[1,32,32,768]{3,2,0,1:T(8,128)(2,1)} %get-tuple-element.79) | copy-start | bytes 4718596
  805.1 279.8 %reduce-scatter.7.cloned.1.call-start = ((), (), s32[]{:S(2)}) async-start(), calls=%async_computation.16 | async-start | bytes 2433024 | tf_op jit(solution)/shard_map/reduce_scatter | solution.py:350
  837.0 366.3 %reduce-scatter.17.cloned.1.call-start = ((), (), s32[]{:S(2)}) async-start(), calls=%async_computation.21 | async-start | bytes 9732096 | tf_op jit(solution)/shard_map/reduce_scatter | solution.py:361
  856.8 488.3 %reduce-scatter.15.cloned.1.call-start = ((), (), s32[]{:S(2)}) async-start(), calls=%async_computation.20 | async-start | bytes 9732096 | tf_op jit(solution)/shard_map/reduce_scatter | solution.py:359
  884.6 82.8 %all-to-all-start.1 = ((bf16[2,1024,768]{2,0,1:T(2,128)(2,1)}), bf16[2,1024,768]{2,0,1:T(2,128)(2,1)}, u32[]{:S(2)}, u32[]{:S(2)}) async-start(bf16[2,1024,768]{2,0,1:T(2,128)(2,1)} %copy.88), calls=%async_computation.1 | async-start | bytes 6291456 | tf_op jit(solution)/shard_map/all_to_all | solution.py:371
  908.6 62.2 %copy-start.96 = (f32[768]{0:T(1024)S(1)}, f32[768]{0:T(1024)}, u32[]{:S(2)}) copy-start(f32[768]{0:T(1024)} %get-tuple-element.27) | copy-start | bytes 9220
  908.6 62.2 %copy-start.97 = (f32[768]{0:T(1024)S(1)}, f32[768]{0:T(1024)}, u32[]{:S(2)}) copy-start(f32[768]{0:T(1024)} %get-tuple-element.30) | copy-start | bytes 9220
  908.6 62.3 %copy-start.114 = (f32[12,64]{1,0:T(8,128)S(1)}, f32[12,64]{1,0:T(8,128)}, u32[]{:S(2)}) copy-start(f32[12,64]{1,0:T(8,128)} %get-tuple-element.125) | copy-start | bytes 9220
  908.6 62.3 %copy-start.115 = (f32[12,64]{1,0:T(8,128)S(1)}, f32[12,64]{1,0:T(8,128)}, u32[]{:S(2)}) copy-start(f32[12,64]{1,0:T(8,128)} %get-tuple-element.127) | copy-start | bytes 9220
  908.6 62.4 %copy-start.94 = (f32[768]{0:T(1024)S(1)}, f32[768]{0:T(1024)}, u32[]{:S(2)}) copy-start(f32[768]{0:T(1024)} %get-tuple-element.19) | copy-start | bytes 9220
  908.6 62.4 %copy-start.95 = (f32[768]{0:T(1024)S(1)}, f32[768]{0:T(1024)}, u32[]{:S(2)}) copy-start(f32[768]{0:T(1024)} %get-tuple-element.99) | copy-start | bytes 9220
  908.6 62.3 %copy-start.112 = (f32[3072]{0:T(1024)S(1)}, f32[3072]{0:T(1024)}, u32[]{:S(2)}) copy-start(f32[3072]{0:T(1024)} %get-tuple-element.129) | copy-start | bytes 36868
  908.6 62.3 %copy-start.113 = (f32[3072]{0:T(1024)S(1)}, f32[3072]{0:T(1024)}, u32[]{:S(2)}) copy-start(f32[3072]{0:T(1024)} %get-tuple-element.131) | copy-start | bytes 36868
  908.7 62.4 %copy-start.98 = (f32[768]{0:T(1024)S(1)}, f32[768]{0:T(1024)}, u32[]{:S(2)}) copy-start(f32[768]{0:T(1024)} %get-tuple-element.61) | copy-start | bytes 9220
  908.7 62.4 %copy-start.99 = (f32[768]{0:T(1024)S(1)}, f32[768]{0:T(1024)}, u32[]{:S(2)}) copy-start(f32[768]{0:T(1024)} %get-tuple-element.92) | copy-start | bytes 9220
  908.7 62.4 %copy-start.117 = (f32[768]{0:T(1024)S(1)}, f32[768]{0:T(1024)}, u32[]{:S(2)}) copy-start(f32[768]{0:T(1024)} %get-tuple-element.23) | copy-start | bytes 9220
  908.7 62.4 %copy-start.120 = (f32[768]{0:T(1024)S(1)}, f32[768]{0:T(1024)}, u32[]{:S(2)}) copy-start(f32[768]{0:T(1024)} %get-tuple-element.97) | copy-start | bytes 9220
  908.7 62.4 %copy-start.116 = (f32[768]{0:T(1024)S(1)}, f32[768]{0:T(1024)}, u32[]{:S(2)}) copy-start(f32[768]{0:T(1024)} %get-tuple-element.34) | copy-start | bytes 9220
  908.7 62.4 %copy-start.119 = (f32[768]{0:T(1024)S(1)}, f32[768]{0:T(1024)}, u32[]{:S(2)}) copy-start(f32[768]{0:T(1024)} %get-tuple-element.94) | copy-start | bytes 9220
  908.7 62.4 %copy-start.100 = (f32[768]{0:T(1024)S(1)}, f32[768]{0:T(1024)}, u32[]{:S(2)}) copy-start(f32[768]{0:T(1024)} %get-tuple-element.65) | copy-start | bytes 9220
  908.7 62.4 %copy-start.118 = (f32[768]{0:T(1024)S(1)}, f32[768]{0:T(1024)}, u32[]{:S(2)}) copy-start(f32[768]{0:T(1024)} %get-tuple-element.67) | copy-start | bytes 9220
  967.4 115.1 %all-to-all-start.3 = ((bf16[2,1024,768]{2,0,1:T(2,128)(2,1)}), bf16[2,1024,768]{2,0,1:T(2,128)(2,1)S(1)}, u32[]{:S(2)}, u32[]{:S(2)}) async-start(bf16[2,1024,768]{2,0,1:T(2,128)(2,1)} %copy.101), calls=%async_computation.3 | async-start | bytes 6291456 | tf_op jit(solution)/shard_map/all_to_all | solution.py:374
  1083.0 262.1 %copy-start.1 = (bf16[64,32,768]{2,1,0:T(8,128)(2,1)S(1)}, bf16[64,32,768]{2,1,0:T(8,128)(2,1)}, u32[]{:S(2)}) copy-start(bf16[64,32,768]{2,1,0:T(8,128)(2,1)} %param.19) | copy-start | bytes 9437188
  (101 other events, 475.6 us)
Sparse Core Ops, SparseCore 0:
  10.9 72.4 all-gather.8
  86.4 53.6 all-gather.10
  143.0 64.4 all-gather.6
  210.3 54.2 all-gather.12
  267.3 62.5 all-gather.14
  332.6 62.4 all-gather.16
  525.5 99.0 reduce-scatter.12
  729.6 99.0 reduce-scatter.10
  834.5 110.6 reduce-scatter.8
  951.8 110.2 reduce-scatter.6
  1068.6 134.6 reduce-scatter.16
  1210.6 134.4 reduce-scatter.14
where the time goes:
time: 1360 us; the launch traced here: 1350 us
  matrix products  564 us (41%)
  waiting for transfers between devices  335 us (25%)
  blocking collectives  193 us (14%)
  other arithmetic  152 us (11%)
  local copies, waits for them, and re-layouts  70.5 us (5%)
  starting transfers between devices  21.3 us (2%)
  between operations  16.5 us (1%)
    unnamed x2, blocking collectives  193 us
    reduce_scatter x1, waiting for transfers between devices, body(): lax.psum_scatter(grads[9], 'dp', scatter_dimension=0, tiled=True)  142 us
    reduce_scatter x1, waiting for transfers between devices, body(): lax.psum_scatter(grads[11], 'dp', scatter_dimension=0, tiled=True)  118 us
    dot_general x12, matrix products, matmul(): return jnp.dot(left, right, preferred_element_type=jnp.float32)  114 us
    dot_general x4, matrix products, attend_back(): jnp.einsum('qhd,khd->hqk', grad_block, value_heads, preferred_element_typ...  93 us
    convert_element_type x2, other arithmetic, attend_back(): grad_scores = (probs * (grad_probs - inner_sum)).astype(jnp.bfloat16)  85.2 us
    dot_general x12, matrix products, matmul_nt(): lax.dot_general(left, right, (((1,), (1,)), ((), ())), preferred_element_...  79.2 us
    dot_general x4, matrix products, attend(): jnp.einsum('qhd,khd->hqk', query_block, key_heads, preferred_element_type...  65 us
  transfers between devices with their start and end apart: 16, of which 4 were waited for; matrix products, arithmetic and copies ran while one was open for 49% of the time, Pallas kernels for 0%

commit v1 on v0

v1 whole, which is shorter than its diff:
```python
import functools
import math

import jax
import jax.numpy as jnp
from jax import lax
from jax.experimental import pallas as pl
from jax.experimental.pallas import tpu as pltpu
from jax.sharding import PartitionSpec as P

F32 = jnp.float32
BF16 = jnp.bfloat16
MESH = pl.DeviceIdType.MESH
ANY = pl.BlockSpec(memory_space=pl.ANY)

HEADS = 12
D = 768
FF = 3072
WIDE = 3 * D
T = 1024
SUB = 32
B = 256
RP = 2816
SLOTS = 4
EPS = 1e-05
LOG2E = 1.4426950408889634
SCALE = 64 ** (-0.5)
SC2 = SCALE * LOG2E

GROUP_PLANE = (2, 3, 1, 0, 0, 1, 0, 0)
GROUP_SLOT = (0, 0, 0, 0, 1, 1, 2, 3)
GROUP_TURN = (False, False, False, False, True, True, False, True)
CAPS = (
    (4, 4, 4, 3, 2, 2, 1, 1),
    (4, 4, 4, 3, 2, 2, 2, 2),
    (4, 4, 4, 4, 4, 4, 4, 4),
)


def dot(left, right):
    return jnp.dot(left, right, preferred_element_type=F32)


def dot_nt(left, right):
    return lax.dot_general(left, right, (((1,), (1,)), ((), ())), preferred_element_type=F32)


def dot_tn(left, right):
    return lax.dot_general(left, right, (((0,), (0,)), ((), ())), preferred_element_type=F32)


def al(x, k):
    return pl.multiple_of(x, k)


def group_device(g, i, quarter):
    place = (quarter - 1 - i) if GROUP_TURN[g] else i
    return GROUP_PLANE[g] * quarter + place


def plane_groups(plane):
    return [g for g in range(8) if GROUP_PLANE[g] == plane]


def sort_kernel(seq_ref, slot_ref, tok, cot, tok_o, cot_o, sem):
    count = tok.shape[0]

    def copies(r):
        return (
            pltpu.make_async_copy(tok.at[seq_ref[r]], tok_o.at[r], sem.at[0]),
            pltpu.make_async_copy(cot.at[slot_ref[r]], cot_o.at[r], sem.at[1]),
        )

    def start(r, _):
        for c in copies(r):
            c.start()
        return 0

    def wait(r, _):
        for c in copies(r):
            c.wait()
        return 0

    lax.fori_loop(0, count, start, 0)
    lax.fori_loop(0, count, wait, 0)


def sort_blocks(seq_of_rank, slot_of_rank, tokens, cotangent):
    return pl.pallas_call(
        sort_kernel,
        grid_spec=pltpu.PrefetchScalarGridSpec(
            num_scalar_prefetch=2,
            grid=(),
            in_specs=[ANY, ANY],
            out_specs=[ANY, ANY],
            scratch_shapes=[pltpu.SemaphoreType.DMA((2,))],
        ),
        out_shape=[jax.ShapeDtypeStruct(tokens.shape, BF16)] * 2,
        name="sort_blocks",
    )(seq_of_rank, slot_of_rank, tokens, cotangent)


def unsort_kernel(rank_ref, live_ref, y, o, zero, sem):
    count = o.shape[0]
    zero[...] = jnp.zeros_like(zero)

    def start(j, _):
        @pl.when(live_ref[j] > 0)
        def _():
            pltpu.make_async_copy(y.at[rank_ref[j]], o.at[j], sem.at[0]).start()

        @pl.when(live_ref[j] <= 0)
        def _():
            pltpu.make_async_copy(zero, o.at[j], sem.at[0]).start()

        return 0

    def wait(j, _):
        pltpu.make_async_copy(zero, o.at[j], sem.at[0]).wait()
        return 0

    lax.fori_loop(0, count, start, 0)
    lax.fori_loop(0, count, wait, 0)


def unsort_blocks(rank_of_slot, live, y):
    return pl.pallas_call(
        unsort_kernel,
        grid_spec=pltpu.PrefetchScalarGridSpec(
            num_scalar_prefetch=2,
            grid=(),
            in_specs=[ANY],
            out_specs=ANY,
            scratch_shapes=[pltpu.VMEM(y.shape[1:], BF16), pltpu.SemaphoreType.DMA((1,))],
        ),
        out_shape=jax.ShapeDtypeStruct(y.shape, BF16),
        name="unsort_blocks",
    )(rank_of_slot, live, y)


def meet(n):
    me = lax.axis_index("dp")
    barrier = pltpu.get_barrier_semaphore()

    def signal(k, _):
        pl.semaphore_signal(barrier, inc=1, device_id=(lax.rem(me + k, n),), device_id_type=MESH)
        return 0

    lax.fori_loop(1, n, signal, 0)
    pl.semaphore_wait(barrier, n - 1)


def deal_kernel(n, caps, x, o, send, recv):
    quarter = n // 4
    rows = x.shape[1]
    me = lax.axis_index("dp")
    plane = me // quarter
    meet(n)
    for g in range(8):
        slot = GROUP_SLOT[g]
        place = o.at[slot, pl.ds(al(me * rows, 8), rows)]

        def start(i, _, g=g, slot=slot, place=place):
            to = group_device(g, i, quarter)
            block = x.at[g * quarter + i]

            @pl.when(to == me)
            def _():
                pltpu.make_async_copy(block, place, recv.at[slot]).start()

            @pl.when(to != me)
            def _():
                pltpu.make_async_remote_copy(
                    block, place, send, recv.at[slot], device_id=(to,), device_id_type=MESH
                ).start()

            return 0

        @pl.when(plane < caps[g])
        def _(start=start):
            lax.fori_loop(0, quarter, start, 0)

    for p in range(4):
        mine = plane_groups(p)
        sent = sum(quarter for g in range(8) if p < caps[g]) - sum(1 for g in mine if p < caps[g])

        @pl.when(plane == p)
        def _(mine=mine, sent=sent):
            for g in mine:
                slot = GROUP_SLOT[g]
                whole = o.at[slot, pl.ds(0, caps[g] * quarter * rows)]
                pltpu.make_async_copy(whole, whole, recv.at[slot]).wait()
            if sent:
                pltpu.make_async_copy(x.at[pl.ds(0, sent)], x.at[pl.ds(0, sent)], send).wait()


def deal(x, n, caps, collective_id):
    return pl.pallas_call(
        functools.partial(deal_kernel, n, caps),
        in_specs=[ANY],
        out_specs=ANY,
        out_shape=jax.ShapeDtypeStruct((SLOTS, T, D), BF16),
        scratch_shapes=[pltpu.SemaphoreType.DMA, pltpu.SemaphoreType.DMA((SLOTS,))],
        compiler_params=pltpu.CompilerParams(collective_id=collective_id, has_side_effects=True),
        name="deal",
    )(x)


def collect_kernel(n, caps, x, o, send, recv):
    quarter = n // 4
    rows = o.shape[1]
    me = lax.axis_index("dp")
    plane = me // quarter
    place = lax.rem(me, quarter)
    meet(n)
    for p in range(4):

        @pl.when(plane == p)
        def _(p=p):
            for g in plane_groups(p):
                slot = GROUP_SLOT[g]
                i = (quarter - 1 - place) if GROUP_TURN[g] else place
                rank = g * quarter + i

                def start(k, _, slot=slot, rank=rank):
                    block = x.at[slot, pl.ds(al(k * rows, 8), rows)]

                    @pl.when(k == me)
                    def _():
                        pltpu.make_async_copy(block, o.at[rank], recv).start()

                    @pl.when(k != me)
                    def _():
                        pltpu.make_async_remote_copy(
                            block, o.at[rank], send, recv, device_id=(k,), device_id_type=MESH
                        ).start()

                    return 0

                lax.fori_loop(0, caps[g] * quarter, start, 0)

    for p in range(4):
        mine = plane_groups(p)
        got = sum(quarter for g in range(8) if p < caps[g])
        sent = sum(caps[g] * quarter for g in mine) - sum(1 for g in mine if p < caps[g])

        @pl.when(plane == p)
        def _(got=got, sent=sent):
            whole = o.at[pl.ds(0, got)]
            pltpu.make_async_copy(whole, whole, recv).wait()
            left = sent
            for slot in range(SLOTS):
                now = min(left, n)
                if now:
                    part = x.at[slot, pl.ds(0, now * rows)]
                    pltpu.make_async_copy(part, part, send).wait()
                left -= now


def collect(x, n, nseq, rows, caps, collective_id):
    return pl.pallas_call(
        functools.partial(collect_kernel, n, caps),
        in_specs=[ANY],
        out_specs=ANY,
        out_shape=jax.ShapeDtypeStruct((nseq, rows, D), BF16),
        scratch_shapes=[pltpu.SemaphoreType.DMA, pltpu.SemaphoreType.DMA],
        compiler_params=pltpu.CompilerParams(collective_id=collective_id, has_side_effects=True),
        name="collect",
    )(x)


def attend_kernel(
    lens, offs, tot, x, w, bias, rows_o, qkv_o, ctx_o, lse_o, rows_v, qkv_v, ctx_v, lse_v, sem_in, sem_out
):
    total = al(tot[0], SUB)
    blocks = tot[1]

    def pieces(act):
        for s in range(SLOTS):
            off = offs[s]

            def one(j, _, s=s, off=off):
                act(
                    pltpu.make_async_copy(
                        x.at[s, pl.ds(al(j * SUB, SUB), SUB)],
                        rows_v.at[pl.ds(al(off + j * SUB, SUB), SUB)],
                        sem_in,
                    )
                )
                return 0

            lax.fori_loop(0, (lens[s] + SUB - 1) // SUB, one, 0)

    pieces(lambda c: c.start())
    rows_v[pl.ds(total, B), :] = jnp.zeros((B, D), BF16)
    qkv_v[pl.ds(al(blocks * B, B), B), :] = jnp.zeros((B, WIDE), BF16)
    pieces(lambda c: c.wait())

    def outs(b):
        at = pl.ds(al(b * B, B), B)
        return (
            pltpu.make_async_copy(rows_v.at[at], rows_o.at[at], sem_out.at[0]),
            pltpu.make_async_copy(qkv_v.at[at], qkv_o.at[at], sem_out.at[1]),
        )

    def project(b, _):
        at = pl.ds(al(b * B, B), B)
        for part in range(3):
            cols = slice(part * D, (part + 1) * D)
            qkv_v[at, cols] = (dot(rows_v[at, :], w[:, cols]) + bias[:, cols]).astype(BF16)
        for c in outs(b):
            c.start()
        return 0

    lax.fori_loop(0, blocks, project, 0)

    lane = lax.broadcasted_iota(jnp.int32, (B, 128), 1)
    column = lax.broadcasted_iota(jnp.int32, (B, B), 1)

    def sequence(s, _):
        length = lens[s]
        off = offs[s]
        spans = (length + B - 1) // B

        def attend(q, t):
            r0 = al(off + q * B, SUB)

            def pair(p, lse):
                c0 = al(p * 128, 128)
                qp = qkv_v[pl.ds(r0, B), pl.ds(c0, 128)]
                ks = [qkv_v[pl.ds(al(off + j * B, SUB), B), pl.ds(al(D + p * 128, 128), 128)] for j in range(t)]
                vs = [qkv_v[pl.ds(al(off + j * B, SUB), B), pl.ds(al(2 * D + p * 128, 128), 128)] for j in range(t)]
                done = []
                for h in range(2):
                    half = (lane < 64) if h == 0 else (lane >= 64)
                    qm = jnp.where(half, qp, jnp.zeros_like(qp))
                    ss = [dot_nt(qm, k) for k in ks]
                    ss[-1] = jnp.where(column < length - (t - 1) * B, ss[-1], -1e30)
                    top = functools.reduce(jnp.maximum, ss)
                    top = jnp.max(top, axis=1, keepdims=True)
                    ps = [jnp.exp2((sc - top) * SC2) for sc in ss]
                    summed = jnp.sum(functools.reduce(jnp.add, ps), axis=1, keepdims=True)
                    o = functools.reduce(jnp.add, [dot(pr.astype(BF16), v) for pr, v in zip(ps, vs)])
                    done.append(o * (1.0 / summed))
                    lse = jnp.where(lane == 2 * p + h, top * SC2 + jnp.log(summed) * LOG2E, lse)
                ctx_v[pl.ds(r0, B), pl.ds(c0, 128)] = jnp.where(lane < 64, done[0], done[1]).astype(BF16)
                return lse

            lse_v[pl.ds(r0, B), :] = lax.fori_loop(0, HEADS // 2, pair, jnp.zeros((B, 128), F32))

        def query_block(q, _):
            for t in range(1, T // B + 1):

                @pl.when(spans == t)
                def _(t=t):
                    attend(q, t)

            return 0

        lax.fori_loop(0, spans, query_block, 0)
        return 0

    lax.fori_loop(0, SLOTS, sequence, 0)
    ctx_v[pl.ds(total, B), :] = jnp.zeros((B, D), BF16)

    def more(b):
        at = pl.ds(al(b * B, B), B)
        return (
            pltpu.make_async_copy(ctx_v.at[at], ctx_o.at[at], sem_out.at[2]),
            pltpu.make_async_copy(lse_v.at[at], lse_o.at[at], sem_out.at[3]),
        )

    def start_more(b, _):
        for c in more(b):
            c.start()
        return 0

    def finish(b, _):
        for c in outs(b) + more(b):
            c.wait()
        return 0

    lax.fori_loop(0, blocks, start_more, 0)
    lax.fori_loop(0, blocks, finish, 0)


def attend(lens, offs, tot, x, w, bias):
    shapes = [((RP, D), BF16), ((RP, WIDE), BF16), ((RP, D), BF16), ((RP, 128), F32)]
    return pl.pallas_call(
        attend_kernel,
        grid_spec=pltpu.PrefetchScalarGridSpec(
            num_scalar_prefetch=3,
            grid=(),
            in_specs=[ANY, pl.BlockSpec(memory_space=pltpu.VMEM), pl.BlockSpec(memory_space=pltpu.VMEM)],
            out_specs=[ANY] * 4,
            scratch_shapes=[pltpu.VMEM(s, d) for s, d in shapes]
            + [pltpu.SemaphoreType.DMA, pltpu.SemaphoreType.DMA((4,))],
        ),
        out_shape=[jax.ShapeDtypeStruct(s, d) for s, d in shapes],
        compiler_params=pltpu.CompilerParams(vmem_limit_bytes=60 << 20),
        name="attend",
    )(lens, offs, tot, x, w, bias)


def live_mask(live, b):
    row = lax.broadcasted_iota(jnp.int32, (B, 1), 0)
    keep = None
    for k in range(B // SUB):
        here = (row >= k * SUB) & (row < k * SUB + live[b * (B // SUB) + k])
        keep = here if keep is None else keep | here
    return keep


def norm(hidden):
    center = hidden - jnp.mean(hidden, axis=-1, keepdims=True)
    scale = lax.rsqrt(jnp.mean(center * center, axis=-1, keepdims=True) + EPS)
    return center * scale, scale


def norm_back(e, normed, scale):
    first = jnp.mean(e, axis=-1, keepdims=True)
    second = jnp.mean(e * normed, axis=-1, keepdims=True)
    return scale * (e - first - normed * second)


def rows_kernel(
    tot, sslot, spos, live, *refs
):
    @pl.when(pl.program_id(0) < tot[1])
    def _():
        rows_block(tot, sslot, spos, live, *refs)


def rows_block(
    tot, sslot, spos, live, rows, ctx, cot, wo, wi, wu, vec, bi,
    out_o, ga_o, gc_o, dd_o, gwo_o, gwi_o, gwu_o, gvec_o, gbi_o,
    cot_v, out_v, act_v, dg_v, gwo, gwi, gwu, gvec, gbi, stage, sem_c, sem_o, sem_w,
):
    b = pl.program_id(0)
    nb = tot[1]
    subs = B // SUB

    def cot_copies(step, act):
        buf = lax.rem(step, 2)
        for k in range(subs):
            at = step * subs + k
            act(
                pltpu.make_async_copy(
                    cot.at[sslot[at], pl.ds(al(spos[at], SUB), SUB)],
                    cot_v.at[buf, pl.ds(k * SUB, SUB)],
                    sem_c.at[buf],
                )
            )

    @pl.when(b == 0)
    def _():
        cot_copies(b, lambda c: c.start())
        gwo[...] = jnp.zeros_like(gwo)
        gwi[...] = jnp.zeros_like(gwi)
        gwu[...] = jnp.zeros_like(gwu)
        gvec[...] = jnp.zeros_like(gvec)
        gbi[...] = jnp.zeros_like(gbi)

    @pl.when(b + 1 < nb)
    def _():
        cot_copies(b + 1, lambda c: c.start())

    bo, g1, s1, bu, g2, s2 = [vec[k : k + 1, :] for k in range(6)]
    x = rows[...].astype(F32)
    c = ctx[...]
    n1, sc1 = norm(x + (dot(c, wo[...]) + bo))
    mixed = n1 * g1 + s1
    low = mixed.astype(BF16)

    def forward(k, branch):
        at = pl.ds(al(k * D, D), D)
        inner = dot(low, wi[:, at]) + bi[:, at]
        half = 0.5 + 0.5 * lax.erf(inner * (0.5**0.5))
        act = (inner * half).astype(BF16)
        act_v[:, at] = act
        dg_v[:, at] = half + inner * (jnp.exp2(inner * inner * (-0.5 * LOG2E)) * (1.0 / math.sqrt(2 * math.pi)))
        return branch + dot(act, wu[at, :])

    branch = lax.fori_loop(0, FF // D, forward, jnp.zeros((B, D), F32))
    n2, sc2 = norm(mixed + (branch + bu))
    keep = live_mask(live, b)
    out_v[...] = jnp.where(keep, n2 * g2 + s2, 0.0).astype(BF16)

    def out_copies(act):
        for k in range(subs):
            at = b * subs + k

            @pl.when(live[at] > 0)
            def _(k=k, at=at):
                act(
                    pltpu.make_async_copy(
                        out_v.at[pl.ds(k * SUB, SUB)],
                        out_o.at[sslot[at], pl.ds(al(spos[at], SUB), SUB)],
                        sem_o,
                    )
                )

    out_copies(lambda cp: cp.start())
    cot_copies(b, lambda cp: cp.wait())
    go = jnp.where(keep, cot_v[lax.rem(b, 2)].astype(F32), 0.0)
    gvec[4:5, :] += jnp.sum(go * n2, axis=0, keepdims=True)
    gvec[5:6, :] += jnp.sum(go, axis=0, keepdims=True)
    gs = norm_back(go * g2, n2, sc2)
    gb = gs.astype(BF16)
    gvec[3:4, :] += jnp.sum(gb.astype(F32), axis=0, keepdims=True)

    def backward(k, gm):
        at = pl.ds(al(k * D, D), D)
        gi = (dot_nt(gb, wu[at, :]) * dg_v[:, at]).astype(BF16)
        gbi[:, at] += jnp.sum(gi.astype(F32), axis=0, keepdims=True)
        gwu[at, :] += dot_tn(act_v[:, at], gb)
        gwi[:, at] += dot_tn(low, gi)
        return gm + dot_nt(gi, wi[:, at])

    gm = lax.fori_loop(0, FF // D, backward, gs)
    gvec[1:2, :] += jnp.sum(gm * n1, axis=0, keepdims=True)
    gvec[2:3, :] += jnp.sum(gm, axis=0, keepdims=True)
    ga = norm_back(gm * g1, n1, sc1).astype(BF16)
    ga_o[...] = ga
    gvec[0:1, :] += jnp.sum(ga.astype(F32), axis=0, keepdims=True)
    gwo[...] += dot_tn(c, ga)
    gc = dot_nt(ga, wo[...]).astype(BF16)
    gc_o[...] = gc
    prod = gc.astype(F32) * c.astype(F32)
    high = prod.astype(BF16)
    rest = (prod - high.astype(F32)).astype(BF16)
    heads = (
        lax.broadcasted_iota(jnp.int32, (D, 128), 0) // 64 == lax.broadcasted_iota(jnp.int32, (D, 128), 1)
    ).astype(BF16)
    dd_o[...] = dot(high, heads) + dot(rest, heads)
    out_copies(lambda cp: cp.wait())

    @pl.when(b == nb - 1)
    def _():
        gvec_o[...] = gvec[...]
        gbi_o[...] = gbi[...]
        stage[0] = gwo[...].astype(BF16)
        copies = [pltpu.make_async_copy(stage.at[0], gwo_o, sem_w.at[0])]
        copies[0].start()
        for k in range(4):
            buf = (k + 1) % 2
            if k:
                copies[k - 1].wait()
            stage[buf] = gwu[k * D : (k + 1) * D, :].astype(BF16)
            copies.append(pltpu.make_async_copy(stage.at[buf], gwu_o.at[pl.ds(k * D, D)], sem_w.at[buf]))
            copies[-1].start()
        for k in range(4):
            buf = (k + 5) % 2
            copies[k + 3].wait()
            stage[buf] = gwi[:, k * D : (k + 1) * D].astype(BF16)
            copies.append(pltpu.make_async_copy(stage.at[buf], gwi_o.at[:, pl.ds(k * D, D)], sem_w.at[buf]))
            copies[-1].start()
        copies[-2].wait()
        copies[-1].wait()


def row_by_row(tot, sslot, spos, live, rows, ctx, cot, wo, wi, wu, vec, bi):
    def at(b, tot, *_):
        return (jnp.minimum(b, tot[1] - 1), 0)

    block = pl.BlockSpec((B, D), at)
    whole = pl.BlockSpec(memory_space=pltpu.VMEM)
    return pl.pallas_call(
        rows_kernel,
        grid_spec=pltpu.PrefetchScalarGridSpec(
            num_scalar_prefetch=4,
            grid=(RP // B,),
            in_specs=[block, block, ANY, whole, whole, whole, whole, whole],
            out_specs=[ANY, block, block, pl.BlockSpec((B, 128), at), ANY, ANY, ANY, whole, whole],
            scratch_shapes=[
                pltpu.VMEM((2, B, D), BF16),
                pltpu.VMEM((B, D), BF16),
                pltpu.VMEM((B, FF), BF16),
                pltpu.VMEM((B, FF), F32),
                pltpu.VMEM((D, D), F32),
                pltpu.VMEM((D, FF), F32),
                pltpu.VMEM((FF, D), F32),
                pltpu.VMEM((8, D), F32),
                pltpu.VMEM((1, FF), F32),
                pltpu.VMEM((2, D, D), BF16),
                pltpu.SemaphoreType.DMA((2,)),
                pltpu.SemaphoreType.DMA,
                pltpu.SemaphoreType.DMA((2,)),
            ],
        ),
        out_shape=[
            jax.ShapeDtypeStruct((SLOTS, T, D), BF16),
            jax.ShapeDtypeStruct((RP, D), BF16),
            jax.ShapeDtypeStruct((RP, D), BF16),
            jax.ShapeDtypeStruct((RP, 128), F32),
            jax.ShapeDtypeStruct((D, D), BF16),
            jax.ShapeDtypeStruct((D, FF), BF16),
            jax.ShapeDtypeStruct((FF, D), BF16),
            jax.ShapeDtypeStruct((8, D), F32),
            jax.ShapeDtypeStruct((1, FF), F32),
        ],
        compiler_params=pltpu.CompilerParams(
            vmem_limit_bytes=60 << 20, dimension_semantics=("arbitrary",)
        ),
        name="row_by_row",
    )(tot, sslot, spos, live, rows, ctx, cot, wo, wi, wu, vec, bi)


def back_kernel(
    lens, offs, tot, sslot, spos, live, rows, qkv, gc, ga, lse, dd, w,
    gin_o, gw_o, gb_o,
    rows_v, qkv_v, gc_v, ga_v, lse_v, dd_v, dk, dv, gw, gb, gin_v, stage, sem_in, sem_g, sem_w,
):
    blocks = tot[1]
    arrays = ((qkv, qkv_v), (gc, gc_v), (lse, lse_v), (dd, dd_v), (rows, rows_v), (ga, ga_v))

    def loads(b, act):
        at = pl.ds(al(b * B, B), B)
        for k, (hbm, vmem) in enumerate(arrays):
            act(pltpu.make_async_copy(hbm.at[at], vmem.at[at], sem_in.at[k]))

    def start_load(b, _):
        loads(b, lambda c: c.start())
        return 0

    def wait_load(b, _):
        loads(b, lambda c: c.wait())
        return 0

    lax.fori_loop(0, blocks, start_load, 0)
    qkv_v[pl.ds(al(blocks * B, B), B), :] = jnp.zeros((B, WIDE), BF16)
    tail = pl.ds(al(blocks * B, B), B)
    gc_v[tail, :] = jnp.zeros((B, D), BF16)
    lse_v[tail, :] = jnp.zeros((B, 128), F32)
    dd_v[tail, :] = jnp.zeros((B, 128), F32)
    gw[...] = jnp.zeros_like(gw)
    gb[...] = jnp.zeros_like(gb)
    lax.fori_loop(0, blocks, wait_load, 0)

    lane = lax.broadcasted_iota(jnp.int32, (B, 128), 1)
    row = lax.broadcasted_iota(jnp.int32, (B, 128), 0)
    key_row = lax.broadcasted_iota(jnp.int32, (B, B), 0)

    def sequence(s, _):
        length = lens[s]
        off = offs[s]
        spans = (length + B - 1) // B

        def pair(p, t):
            c0 = al(p * 128, 128)
            kc = pl.ds(al(D + p * 128, 128), 128)
            vc = pl.ds(al(2 * D + p * 128, 128), 128)
            for j in range(t):
                dk[j] = jnp.zeros((B, 128), F32)
                dv[j] = jnp.zeros((B, 128), F32)

            def query_block(q, _):
                r0 = al(off + q * B, SUB)
                at = pl.ds(r0, B)
                qp = qkv_v[at, pl.ds(c0, 128)]
                fresh = row < length - q * B
                gp = jnp.where(fresh, gc_v[at, pl.ds(c0, 128)], jnp.zeros((B, 128), BF16))
                lse_t = jnp.transpose(lse_v[at, :])
                dd_t = jnp.transpose(jnp.where(fresh, dd_v[at, :], 0.0))
                head = lax.broadcasted_iota(jnp.int32, (128, B), 0)
                dq = jnp.zeros((B, 128), F32)
                for h in range(2):
                    half = (lane < 64) if h == 0 else (lane >= 64)
                    qm = jnp.where(half, qp, jnp.zeros_like(qp))
                    gm = jnp.where(half, gp, jnp.zeros_like(gp))
                    mine = head == 2 * p + h
                    lse_h = jnp.sum(jnp.where(mine, lse_t, 0.0), axis=0, keepdims=True)
                    dd_h = jnp.sum(jnp.where(mine, dd_t, 0.0), axis=0, keepdims=True)
                    for j in range(t):
                        kat = pl.ds(al(off + j * B, SUB), B)
                        k = qkv_v[kat, kc]
                        v = qkv_v[kat, vc]
                        pt = jnp.exp2(dot_nt(k, qm) * SC2 - lse_h)
                        if j == t - 1:
                            pt = jnp.where(key_row < length - j * B, pt, 0.0)
                        dv[j] += dot(pt.astype(BF16), gm)
                        ds = (pt * (dot_nt(v, gm) - dd_h)).astype(BF16)
                        dk[j] += dot(ds, qm)
                        dq += dot_tn(ds, jnp.where(half, k, jnp.zeros_like(k)))
                qkv_v[at, pl.ds(c0, 128)] = jnp.where(fresh, (dq * SCALE).astype(BF16), qp)
                return 0

            lax.fori_loop(0, spans, query_block, 0)
            for j in range(t):
                kat = pl.ds(al(off + j * B, SUB), B)
                fresh = row < length - j * B
                qkv_v[kat, kc] = jnp.where(fresh, (dk[j] * SCALE).astype(BF16), qkv_v[kat, kc])
                qkv_v[kat, vc] = jnp.where(fresh, dv[j].astype(BF16), qkv_v[kat, vc])

        def pairs(p, _):
            for t in range(1, T // B + 1):

                @pl.when(spans == t)
                def _(t=t):
                    pair(p, t)

            return 0

        lax.fori_loop(0, HEADS // 2, pairs, 0)
        return 0

    lax.fori_loop(0, SLOTS, sequence, 0)
    subs = B // SUB

    def gin_copies(b, act):
        for k in range(subs):
            at = b * subs + k

            @pl.when(live[at] > 0)
            def _(k=k, at=at):
                act(
                    pltpu.make_async_copy(
                        gin_v.at[lax.rem(b, 2), pl.ds(k * SUB, SUB)],
                        gin_o.at[sslot[at], pl.ds(al(spos[at], SUB), SUB)],
                        sem_g.at[lax.rem(b, 2)],
                    )
                )

    def gather(b, _):
        at = pl.ds(al(b * B, B), B)
        keep = live_mask(live, b)
        x = rows_v[at, :]
        total = ga_v[at, :].astype(F32)
        for part in range(3):
            cols = slice(part * D, (part + 1) * D)
            g = jnp.where(keep, qkv_v[at, cols], jnp.zeros((B, D), BF16))
            gb[:, cols] += jnp.sum(g.astype(F32), axis=0, keepdims=True)
            gw[:, cols] += dot_tn(x, g)
            total = total + dot_nt(g, w[:, cols])

        @pl.when(b >= 2)
        def _():
            gin_copies(b - 2, lambda c: c.wait())

        gin_v[lax.rem(b, 2)] = total.astype(BF16)
        gin_copies(b, lambda c: c.start())
        return 0

    lax.fori_loop(0, blocks, gather, 0)
    gb_o[...] = gb[...]
    copies = []
    for part in range(3):
        if part >= 2:
            copies[part - 2].wait()
        cols = slice(part * D, (part + 1) * D)
        stage[part % 2] = gw[:, cols].astype(BF16)
        copies.append(pltpu.make_async_copy(stage.at[part % 2], gw_o.at[part], sem_w.at[part % 2]))
        copies[-1].start()
    for c in copies[1:]:
        c.wait()

    def last(b, _):
        gin_copies(b, lambda c: c.wait())
        return 0

    lax.fori_loop(jnp.maximum(blocks - 2, 0), blocks, last, 0)


def attend_back(lens, offs, tot, sslot, spos, live, rows, qkv, gc, ga, lse, dd, w):
    whole = pl.BlockSpec(memory_space=pltpu.VMEM)
    return pl.pallas_call(
        back_kernel,
        grid_spec=pltpu.PrefetchScalarGridSpec(
            num_scalar_prefetch=6,
            grid=(),
            in_specs=[ANY] * 6 + [whole],
            out_specs=[ANY, ANY, whole],
            scratch_shapes=[
                pltpu.VMEM((RP, D), BF16),
                pltpu.VMEM((RP, WIDE), BF16),
                pltpu.VMEM((RP, D), BF16),
                pltpu.VMEM((RP, D), BF16),
                pltpu.VMEM((RP, 128), F32),
                pltpu.VMEM((RP, 128), F32),
                pltpu.VMEM((T // B, B, 128), F32),
                pltpu.VMEM((T // B, B, 128), F32),
                pltpu.VMEM((D, WIDE), F32),
                pltpu.VMEM((1, WIDE), F32),
                pltpu.VMEM((2, B, D), BF16),
                pltpu.VMEM((2, D, D), BF16),
                pltpu.SemaphoreType.DMA((6,)),
                pltpu.SemaphoreType.DMA((2,)),
                pltpu.SemaphoreType.DMA((2,)),
            ],
        ),
        out_shape=[
            jax.ShapeDtypeStruct((SLOTS, T, D), BF16),
            jax.ShapeDtypeStruct((3, D, D), BF16),
            jax.ShapeDtypeStruct((1, WIDE), F32),
        ],
        compiler_params=pltpu.CompilerParams(vmem_limit_bytes=60 << 20),
        name="attend_back",
    )(lens, offs, tot, sslot, spos, live, rows, qkv, gc, ga, lse, dd, w)


def plan(lengths, order, n, me):
    nseq = lengths.shape[0]
    quarter = n // 4
    ids = lax.iota(jnp.int32, nseq)
    ahead = (lengths[None, :] > lengths[:, None]) | (
        (lengths[None, :] == lengths[:, None]) & (ids[None, :] < ids[:, None])
    )
    rank = jnp.sum(ahead.astype(jnp.int32), axis=1)
    rank_of_slot = jnp.sum(jnp.where(order[:, None] == ids[None, :], rank[None, :], 0), axis=1)
    is_rank = rank[None, :] == ids[:, None]
    seq_of_rank = jnp.sum(jnp.where(is_rank, ids[None, :], 0), axis=1)
    len_of_rank = jnp.sum(jnp.where(is_rank, lengths[None, :], 0), axis=1)
    slot_of_rank = jnp.sum(jnp.where(rank_of_slot[None, :] == ids[:, None], ids[None, :], 0), axis=1)
    len_of_slot = jnp.sum(jnp.where(order[:, None] == ids[None, :], lengths[None, :], 0), axis=1)

    group = ids // quarter
    i = ids % quarter
    dev = jnp.zeros_like(ids)
    slot = jnp.zeros_like(ids)
    for g in range(8):
        dev = jnp.where(group == g, group_device(g, i, quarter), dev)
        slot = jnp.where(group == g, GROUP_SLOT[g], slot)
    mine = (dev == me)[None, :] & (slot[None, :] == lax.iota(jnp.int32, SLOTS)[:, None])
    lens = jnp.sum(jnp.where(mine, len_of_rank[None, :], 0), axis=1)
    subs = (lens + SUB - 1) // SUB
    ends = jnp.sum(
        jnp.where(lax.iota(jnp.int32, SLOTS)[None, :] <= lax.iota(jnp.int32, SLOTS)[:, None], subs[None, :], 0), axis=1
    )
    starts = ends - subs
    total = ends[SLOTS - 1] * SUB
    blocks = (total + B - 1) // B
    k = lax.iota(jnp.int32, RP // SUB)
    inside = (k[:, None] >= starts[None, :]) & (k[:, None] < ends[None, :])
    sslot = jnp.sum(jnp.where(inside, lax.iota(jnp.int32, SLOTS)[None, :], 0), axis=1)
    spos = jnp.sum(jnp.where(inside, (k[:, None] - starts[None, :]) * SUB, 0), axis=1)
    left = jnp.sum(jnp.where(inside, lens[None, :], 0), axis=1)
    live = jnp.clip(left - spos, 0, SUB)

    def fits(caps):
        good = None
        for g in range(8):
            ok = len_of_rank[g * quarter] <= caps[g] * (T // 4)
            good = ok if good is None else good & ok
        return good

    way = jnp.where(fits(CAPS[0]), 0, jnp.where(fits(CAPS[1]), 1, 2)).astype(jnp.int32)
    return dict(
        seq_of_rank=seq_of_rank, slot_of_rank=slot_of_rank, rank_of_slot=rank_of_slot, len_of_slot=len_of_slot,
        lens=lens, offs=starts * SUB, tot=jnp.stack([total, blocks]), sslot=sslot, spos=spos, live=live, way=way,
    )


def body(
    tokens, cotangent, lengths, order, query_weight, query_bias, key_weight, value_weight, value_bias,
    output_weight, output_bias, first_gain, first_shift, inner_weight, inner_bias, outer_weight, outer_bias,
    second_gain, second_shift,
):
    n = lax.axis_size("dp")
    me = lax.axis_index("dp")
    nseq, rows = tokens.shape[:2]
    dr = D // n
    fr = FF // n

    small = [query_bias, value_bias, output_bias, first_gain, first_shift, outer_bias, second_gain, second_shift]
    flat = jnp.concatenate(small + [inner_bias])
    flat = jnp.pad(flat, (0, 8 * D - flat.shape[0])).reshape(8, D)
    inner4 = inner_weight.reshape(dr, 4, D).transpose(1, 0, 2).reshape(4 * dr, D)
    shard = jnp.concatenate([query_weight, key_weight, value_weight, output_weight, inner4, outer_weight, flat], axis=0)
    full = lax.all_gather(shard, "dp", axis=0, tiled=False)

    p = plan(lengths, order, n, me)
    sorted_tokens, sorted_cot = sort_blocks(p["seq_of_rank"], p["slot_of_rank"], tokens, cotangent)

    def dealt(x, first_id):
        return lax.switch(
            p["way"],
            [functools.partial(deal, n=n, caps=CAPS[k], collective_id=first_id + k) for k in range(3)],
            x,
        )

    def collected(x, first_id):
        return lax.switch(
            p["way"],
            [
                functools.partial(collect, n=n, nseq=nseq, rows=rows, caps=CAPS[k], collective_id=first_id + k)
                for k in range(3)
            ],
            x,
        )

    x_in = dealt(sorted_tokens, 0)
    g_in = dealt(sorted_cot, 3)

    def part(lo, count):
        return full[:, lo : lo + count].reshape(n * count, D)

    wq, wk, wv, wo = [part(k * dr, dr) for k in range(4)]
    wi = full[:, 4 * dr : 8 * dr].reshape(n, 4, dr, D).transpose(0, 2, 1, 3).reshape(D, FF)
    wu = part(8 * dr, fr)
    vecs = full[:, 8 * dr + fr :].reshape(n, 8 * D)
    bq, bv, bo, g1, s1, bu, g2, s2 = [vecs[:, k * dr : (k + 1) * dr].reshape(D).astype(F32) for k in range(8)]
    bi = vecs[:, 8 * dr : 8 * dr + fr].reshape(1, FF).astype(F32)
    wqkv = jnp.concatenate([wq, wk, wv], axis=1)
    bqkv = jnp.concatenate([bq, jnp.zeros((D,), F32), bv]).reshape(1, WIDE)
    zero = jnp.zeros((D,), F32)
    vec = jnp.stack([bo, g1, s1, bu, g2, s2, zero, zero])

    packed, qkv, ctx, lse = attend(p["lens"], p["offs"], p["tot"], x_in, wqkv, bqkv)
    out, ga, gc, dd, gwo, gwi, gwu, gvec, gbi = row_by_row(
        p["tot"], p["sslot"], p["spos"], p["live"], packed, ctx, g_in, wo, wi, wu, vec, bi
    )
    y_out = collected(out, 6)
    gin, gqkv, gbqkv = attend_back(
        p["lens"], p["offs"], p["tot"], p["sslot"], p["spos"], p["live"], packed, qkv, gc, ga, lse, dd, wqkv
    )
    y_gin = collected(gin, 9)

    live_here = p["len_of_slot"] - me * rows
    output = unsort_blocks(p["rank_of_slot"], live_here, y_out)
    input_gradient = unsort_blocks(p["rank_of_slot"], live_here, y_gin)

    gq, gk, gv = [gqkv[k].reshape(n, dr, D) for k in range(3)]
    inner_piece = gwi.reshape(n, dr, 4, D).transpose(0, 2, 1, 3).reshape(n, 4 * dr, D)
    vectors = [gbqkv[0, :D], gbqkv[0, 2 * D :], gvec[0], gvec[1], gvec[2], gvec[3], gvec[4], gvec[5]]
    vec_piece = jnp.concatenate([v.reshape(n, dr) for v in vectors] + [gbi.reshape(n, fr)], axis=1).astype(BF16)
    vec_piece = jnp.pad(vec_piece, ((0, 0), (0, 8 * D - vec_piece.shape[1]))).reshape(n, 8, D)
    pieces = jnp.concatenate(
        [gq, gk, gv, gwo.reshape(n, dr, D), inner_piece, gwu.reshape(n, fr, D), vec_piece], axis=1
    )
    summed = lax.psum_scatter(pieces, "dp", scatter_dimension=0, tiled=False).astype(F32)
    sq, sk, sv, so = [summed[k * dr : (k + 1) * dr] for k in range(4)]
    si = summed[4 * dr : 8 * dr].reshape(4, dr, D).transpose(1, 0, 2).reshape(dr, FF)
    su = summed[8 * dr : 8 * dr + fr]
    svec = summed[8 * dr + fr :].reshape(8 * D)
    v = [svec[k * dr : (k + 1) * dr] for k in range(8)]
    sbi = svec[8 * dr : 8 * dr + fr]
    return (
        output, input_gradient, sq, v[0], sk, sv, v[1], so, v[2], v[3], v[4], si, sbi, su, v[5], v[6], v[7],
    )


def solution(mesh):
    matrix, vector = P("dp", None), P("dp")
    token = P(None, "dp", None)
    in_specs = (
        token, token, P(), P(), matrix, vector, matrix, matrix, vector, matrix, vector, vector, vector,
        matrix, vector, matrix, vector, vector, vector,
    )
    out_specs = (
        token, token, matrix, vector, matrix, matrix, vector, matrix, vector, vector, vector,
        matrix, vector, matrix, vector, vector, vector,
    )
    return jax.shard_map(body, mesh=mesh, in_specs=in_specs, out_specs=out_specs, check_vma=False)
```

time: 1360 us -> 718 us (0.53)
  Pallas kernels: 0 us -> 600 us
  matrix products: 564 us -> 0 us
  waiting for transfers between devices: 335 us -> 0.06 us
  blocking collectives: 193 us -> 0 us
  other arithmetic: 152 us -> 12.5 us
  starting transfers between devices: 21.3 us -> 0.08 us
    pallas_call x0 -> x10, Pallas kernels: none -> 600 us  [the longest x2 99.4 us: unsort_blocks(): pl.pallas_call(unsort_kernel, grid_spec=pltpu.PrefetchScalarGridSpec(num_...]
    dot_general x60 -> x0, matrix products: 564 us -> none  [the longest x12 114 us: matmul(): return jnp.dot(left, right, preferred_element_type=jnp.float32)]
    reduce_scatter x6 -> x1, waiting for transfers between devices: 260 us -> 0.02 us  [body(): lax.psum_scatter(pieces, 'dp', scatter_dimension=0, tiled=False).astype(F32)]
    unnamed x2 -> x0, blocking collectives: 193 us -> none
    convert_element_type x17 -> x3, other arithmetic: 100 us -> 2.47 us  [the longest x1 1.08 us: body(): lax.psum_scatter(pieces, 'dp', scatter_dimension=0, tiled=False).astype(F32)]
    all_to_all x4 -> x0, waiting for transfers between devices: 58.7 us -> none  [the longest x1 58.7 us: body(): lax.all_to_all(jnp.concatenate(results, axis=0), 'dp', split_axis=1, conc...]
    reduce_sum x12 -> x6, other arithmetic: 41.8 us -> 3.75 us  [the longest x1 1.38 us: plan(): seq_of_rank = jnp.sum(jnp.where(is_rank, ids[None, :], 0), axis=1)]
    all_to_all x4 -> x0, starting transfers between devices: 19.9 us -> none  [the longest x1 7.3 us: body(): lax.all_to_all(dealt, 'dp', split_axis=0, concat_axis=1, tiled=True)]
  transfers between devices with their start and end apart: 16 -> 2, of which waited for: 4 -> 0; matrix products, arithmetic and copies ran while one was open for 49% -> 1% of each run, Pallas kernels for 0% -> 53%
where the time goes in v1:
time: 718 us; the launch traced here: 715 us
  Pallas kernels  600 us (84%)
  local copies, waits for them, and re-layouts  80.7 us (11%)
  between operations  21.6 us (3%)
  other arithmetic  12.5 us (2%)
    pallas_call x2, Pallas kernels, unsort_blocks(): pl.pallas_call(unsort_kernel, grid_spec=pltpu.PrefetchScalarGridSpec(num_...  99.4 us
    pallas_call x1, Pallas kernels, sort_blocks(): pl.pallas_call(sort_kernel, grid_spec=pltpu.PrefetchScalarGridSpec(num_sc...  97.1 us
    pallas_call x2, Pallas kernels, collect(): pl.pallas_call(functools.partial(collect_kernel, n, caps), in_specs=[ANY]...  96.7 us
    pallas_call x1, Pallas kernels, attend_back(): pl.pallas_call(back_kernel, grid_spec=pltpu.PrefetchScalarGridSpec(num_sc...  87.6 us
    pallas_call x2, Pallas kernels, deal(): pl.pallas_call(functools.partial(deal_kernel, n, caps), in_specs=[ANY], o...  87.4 us
    pallas_call x1, Pallas kernels, row_by_row(): pl.pallas_call(rows_kernel, grid_spec=pltpu.PrefetchScalarGridSpec(num_sc...  84 us
    pallas_call x1, Pallas kernels, attend(): pl.pallas_call(attend_kernel, grid_spec=pltpu.PrefetchScalarGridSpec(num_...  47.6 us
    unnamed x47, local copies, waits for them, and re-layouts  19.9 us
  transfers between devices with their start and end apart: 2, of which 0 were waited for; matrix products, arithmetic and copies ran while one was open for 1% of the time, Pallas kernels for 53%

profile of v1, /device:TPU:0, one launch (start us, length us, event | category | flops | bytes accessed | tf_op | source)
XLA Modules:
  0.0 714.8 jit_solution(11395302390417047853)
XLA Ops:
  7.2 6.1 concatenate.19
  13.4 0.9 copy.54
  14.3 0.8 constant_dynamic-update-slice_fusion.6
  15.1 0.8 constant_dynamic-update-slice_fusion.5
  15.9 0.8 constant_dynamic-update-slice_fusion.4
  16.6 0.8 constant_dynamic-update-slice_fusion.3
  17.4 0.9 constant_dynamic-update-slice_fusion.1
  18.4 0.8 copy-done.2
  19.2 0.9 convert_reduce_fusion
  20.1 1.4 select_reduce_fusion.1
  30.2 0.6 select_reduce_fusion.slot_ref
  30.8 97.1 %sort_blocks.1 = (bf16[64,32,768]{2,1,0:T(8,128)(2,1)}, bf16[64,32,768]{2,1,0:T(8,128)(2,1)S(1)}) custom-call(s32[64]{0:T(128)} %get-tuple-element.92.seq_ref, s32[64]{0:T(128)} %select_reduce_fusion.slot_ref, bf16[64,32,768]{2,1,0:T(8,128)(2,1)} %tok.1, bf16[64,32,768]{2,1,0:T(8,128)(2,1)} %cot.1), custom_call_target="tpu_custom_call" | custom-call | tf_op jit(solution)/shard_map/sort_blocks/pallas_call | solution.py:89
  127.9 44.6 %conditional.4 = (bf16[4,1024,768]{2,1,0:T(8,128)(2,1)}) conditional(s32[]{:T(128)} %bitcast, bf16[64,32,768]{2,1,0:T(8,128)(2,1)} %get-tuple-element.63, bf16[64,32,768]{2,1,0:T(8,128)(2,1)} %get-tuple-element.63, bf16[64,32,768]{2,1,0:T(8,128)(2,1)} %get-tuple-element.63), branch_computations={%region_11.12_spmd, %region_12.13_spmd, %region_13.14_spmd} | conditional | bytes 8 | solution.py:875
  127.9 44.6 %deal.6 = bf16[4,1024,768]{2,1,0:T(8,128)(2,1)} custom-call(bf16[64,32,768]{2,1,0:T(8,128)(2,1)} %x.4), custom_call_target="tpu_custom_call" | custom-call | tf_op jit(solution)/shard_map/cond/branch_0_fun/deal/pallas_call | solution.py:198
  172.5 42.9 %conditional.5 = (bf16[4,1024,768]{2,1,0:T(8,128)(2,1)}) conditional(s32[]{:T(128)} %bitcast, bf16[64,32,768]{2,1,0:T(8,128)(2,1)S(1)} %get-tuple-element.66, bf16[64,32,768]{2,1,0:T(8,128)(2,1)S(1)} %get-tuple-element.66, bf16[64,32,768]{2,1,0:T(8,128)(2,1)S(1)} %get-tuple-element.66), branch_computations={%region_14.15_spmd, %region_15.16_spmd, %region_16.17_spmd} | conditional | bytes 8 | solution.py:875
  172.5 42.8 %deal.9 = bf16[4,1024,768]{2,1,0:T(8,128)(2,1)} custom-call(bf16[64,32,768]{2,1,0:T(8,128)(2,1)S(1)} %x.7), custom_call_target="tpu_custom_call" | custom-call | tf_op jit(solution)/shard_map/cond/branch_0_fun/deal/pallas_call | solution.py:198
  218.2 1.0 slice.249
  219.3 0.7 slice_convert_fusion
  219.9 0.7 slice_convert_fusion.1
  220.7 3.7 fusion.6
  224.3 7.9 %fusion.5 = (bf16[32,96,768]{2,1,0:T(8,128)(2,1)}, bf16[32,96,768]{2,1,0:T(8,128)(2,1)}) fusion(bf16[32,296,768]{2,1,0:T(8,128)(2,1)} %bitcast.55), kind=kLoop, calls=%fused_computation.89 | loop fusion | bytes 18874368 | tf_op jit(solution)/shard_map/slice | solution.py:895
  232.3 1.4 reshape.344.refs_7_
  233.7 1.4 reshape.343
  235.1 1.4 reshape.342
  236.5 1.4 reshape.341
  237.9 1.4 reshape.340
  239.2 1.4 reshape.339
  240.6 1.4 reshape.338
  242.0 1.4 reshape.337
  243.4 0.7 reshape.336
  244.1 0.7 pad_maximum_fusion.1
  245.4 4.7 copy.45
  250.1 3.3 copy.51
  253.4 1.9 pad_maximum_fusion.w
  255.3 47.6 %attend.1 = (bf16[2816,768]{1,0:T(8,128)(2,1)}, bf16[2816,2304]{1,0:T(8,128)(2,1)}, bf16[2816,768]{1,0:T(8,128)(2,1)}, f32[2816,128]{1,0:T(8,128)}) custom-call(s32[4]{0:T(128)} %copy-done.4, s32[4]{0:T(128)} %get-tuple-element.96.offs, s32[2]{0:T(128)} %pad_add_fusion.tot, bf16[4,1024,768]{2,1,0:T(8,128)(2,1)} %get-tuple-element.135.x, ...), custom_call_target="tpu_custom_call" | custom-call | tf_op jit(solution)/shard_map/attend/pallas_call | solution.py:389
  303.1 0.6 stack.22.refs_6_
  303.7 84.0 %row_by_row.1 = (bf16[4,1024,768]{2,1,0:T(8,128)(2,1)}, bf16[2816,768]{1,0:T(8,128)(2,1)}, bf16[2816,768]{1,0:T(8,128)(2,1)}, f32[2816,128]{1,0:T(8,128)}, bf16[...) custom-call(s32[2]{0:T(128)} %pad_add_fusion.tot, ...), custom_call_target="tpu_custom_call" | custom-call | tf_op jit(solution)/shard_map/row_by_row/pallas_call | solution.py:568
  387.7 0.7 convert_reduce_fusion.1
  388.6 87.6 %attend_back.1 = (bf16[4,1024,768]{2,1,0:T(8,128)(2,1)}, bf16[3,768,768]{2,1,0:T(8,128)(2,1)}, f32[1,2304]{1,0:T(1,128)}) custom-call(s32[4]{0:T(128)} %copy-done.4, s32[4]{0:T(128)} %get-tuple-element.96.offs, s32[2]{0:T(128)} %pad_add_fusion.tot, s32[88]{0:T(128)} %get-tuple-element.91.sslot, s32[88]{0:T(128)} %copy-done.11, s32[88]{0:T(128)} %subtract_clamp_fusion.live, ...), custom_call_target="tpu_custom_call" | custom-call | tf_op jit(solution)/shard_map/attend_back/pallas_call | solution.py:766
  476.1 0.7 convert.41
  477.9 0.8 copy.52
  478.7 2.2 fusion.7
  480.9 9.8 %reshape.327 = bf16[32,24,4,768]{3,2,1,0:T(4,128)(2,1)} reshape(bf16[768,3072]{1,0:T(8,128)(2,1)} %get-tuple-element.76) | data formatting | bytes 9437184 | tf_op jit(solution)/shard_map/reshape | solution.py:923
  490.7 3.2 copy.46
  493.9 1.1 constant_dynamic-update-slice_fusion.13
  495.0 1.1 constant_dynamic-update-slice_fusion.12
  496.2 1.2 constant_dynamic-update-slice_fusion.11
  497.4 1.1 constant_dynamic-update-slice_fusion.10
  498.5 2.5 constant_dynamic-update-slice_fusion.9
  501.2 2.4 constant_dynamic-update-slice_fusion.8
  503.7 0.8 constant_dynamic-update-slice_fusion.7
  504.6 0.6 copy-done.13
  505.7 45.2 %conditional.6 = (bf16[64,32,768]{2,1,0:T(8,128)(2,1)S(1)}) conditional(s32[]{:T(128)} %bitcast, bf16[4,1024,768]{2,1,0:T(8,128)(2,1)} %get-tuple-element.67, bf16[4,1024,768]{2,1,0:T(8,128)(2,1)} %get-tuple-element.67, bf16[4,1024,768]{2,1,0:T(8,128)(2,1)} %get-tuple-element.67), branch_computations={%region_17.18_spmd, %region_18.19_spmd, %region_19.20_spmd} | conditional | bytes 8 | solution.py:882
  505.7 45.2 %collect.6 = bf16[64,32,768]{2,1,0:T(8,128)(2,1)S(1)} custom-call(bf16[4,1024,768]{2,1,0:T(8,128)(2,1)} %x.10), custom_call_target="tpu_custom_call" | custom-call | tf_op jit(solution)/shard_map/cond/branch_0_fun/collect/pallas_call | solution.py:261
  550.9 51.5 %conditional.7 = (bf16[64,32,768]{2,1,0:T(8,128)(2,1)}) conditional(s32[]{:T(128)} %bitcast, bf16[4,1024,768]{2,1,0:T(8,128)(2,1)} %get-tuple-element.73, bf16[4,1024,768]{2,1,0:T(8,128)(2,1)} %get-tuple-element.73, bf16[4,1024,768]{2,1,0:T(8,128)(2,1)} %get-tuple-element.73), branch_computations={%region_20.21_spmd, %region_21.22_spmd, %region_22.23_spmd} | conditional | bytes 8 | solution.py:882
  550.9 51.5 %collect.9 = bf16[64,32,768]{2,1,0:T(8,128)(2,1)} custom-call(bf16[4,1024,768]{2,1,0:T(8,128)(2,1)} %x.13), custom_call_target="tpu_custom_call" | custom-call | tf_op jit(solution)/shard_map/cond/branch_0_fun/collect/pallas_call | solution.py:261
  602.4 2.3 unsort_blocks.2
  604.7 97.1 %unsort_blocks.3 = bf16[64,32,768]{2,1,0:T(8,128)(2,1)} custom-call(s32[64]{0:T(128)} %copy-done.12, s32[64]{0:T(128)} %broadcast_subtract_fusion.live_ref, bf16[64,32,768]{2,1,0:T(8,128)(2,1)} %get-tuple-element.138.y), custom_call_target="tpu_custom_call" | custom-call | tf_op jit(solution)/shard_map/unsort_blocks/pallas_call | solution.py:127
  701.9 0.7 slice.271
  703.8 1.1 convert_element_type.126
  704.9 0.7 slice_bitcast_fusion
  705.6 0.7 slice_bitcast_fusion.1
  706.3 0.9 slice.280
  707.2 0.7 copy.49
  (74 shorter events, 8.1 us)
Async XLA Ops:
  7.2 211.0 %all-gather.3.cloned.1.call-start = ((), (), s32[]{:S(2)}) async-start(), calls=%async_computation.2 | async-start | bytes 15003648 | tf_op jit(solution)/shard_map/all_gather | solution.py:869
  18.4 0.8 copy-start.2
  19.1 682.7 %reduce-scatter.2.cloned.1.call-start = ((), (), s32[]{:S(2)}) async-start(), calls=%async_computation.1 | async-start | bytes 15003648 | tf_op jit(solution)/shard_map/reduce_scatter | solution.py:930
  21.5 9.3 %copy-start.12 = (s32[64]{0:T(128)}, s32[64]{0:T(128)S(1)}, u32[]{:S(2)}) copy-start(s32[64]{0:T(128)S(1)} %get-tuple-element.95.rank_ref) | copy-start | bytes 772
  21.6 194.9 %copy-start.4 = (s32[4]{0:T(128)}, s32[4]{0:T(128)S(1)}, u32[]{:S(2)}) copy-start(s32[4]{0:T(128)S(1)} %select_reduce_fusion.9.lens) | copy-start | bytes 52
  217.1 0.5 copy-start.11
  255.3 47.7 %copy-start.5 = (f32[1,768]{1,0:T(1,128)S(1)}, f32[1,768]{1,0:T(1,128)}, u32[]{:S(2)}) copy-start(f32[1,768]{1,0:T(1,128)} %reshape.343) | copy-start | bytes 9220
  255.3 47.7 %copy-start.6 = (f32[1,768]{1,0:T(1,128)S(1)}, f32[1,768]{1,0:T(1,128)}, u32[]{:S(2)}) copy-start(f32[1,768]{1,0:T(1,128)} %reshape.342) | copy-start | bytes 9220
  255.3 47.7 %copy-start.7 = (f32[1,768]{1,0:T(1,128)S(1)}, f32[1,768]{1,0:T(1,128)}, u32[]{:S(2)}) copy-start(f32[1,768]{1,0:T(1,128)} %reshape.341) | copy-start | bytes 9220
  255.3 47.7 %copy-start.8 = (f32[1,768]{1,0:T(1,128)S(1)}, f32[1,768]{1,0:T(1,128)}, u32[]{:S(2)}) copy-start(f32[1,768]{1,0:T(1,128)} %reshape.340) | copy-start | bytes 9220
  255.3 47.7 %copy-start.9 = (f32[1,768]{1,0:T(1,128)S(1)}, f32[1,768]{1,0:T(1,128)}, u32[]{:S(2)}) copy-start(f32[1,768]{1,0:T(1,128)} %reshape.339) | copy-start | bytes 9220
  255.3 47.7 %copy-start.10 = (f32[1,768]{1,0:T(1,128)S(1)}, f32[1,768]{1,0:T(1,128)}, u32[]{:S(2)}) copy-start(f32[1,768]{1,0:T(1,128)} %reshape.338) | copy-start | bytes 9220
  388.6 88.5 %copy-start.3 = (f32[8,768]{1,0:T(8,128)S(1)}, f32[8,768]{1,0:T(8,128)}, u32[]{:S(2)}) copy-start(f32[8,768]{1,0:T(8,128)} %get-tuple-element.79) | copy-start | bytes 73732
  493.9 3.5 copy-start.1
  497.4 3.6 slice-start
  498.5 2.7 slice-start.1
  501.2 2.5 copy-start
  504.5 0.7 copy-start.13
Sparse Core Ops, SparseCore 0:
  19.3 107.6 all-gather.2
  504.7 196.2 reduce-scatter.1
